TPU v7x, 32 devices: a whole 2x2x4 slice. The times are simulated.
32 devices in a mesh: ctx: 16 (over z, y, x), head: 2 (over core).
Axes of the slice: x: 2, y: 2, z: 4, core: 2. Of those that a mesh axis runs over, the one named last changes fastest.
Arguments:
- queries: float32 [8192, 512], P('ctx', 'head'), may hold values from -1024 to 1024
- keys: float32 [8192, 128], P('ctx'), may hold values from -1024 to 1024
- values: float32 [8192, 128], P('ctx'), may hold values from -6 to 6
- cotangent: float32 [8192, 512], P('ctx', 'head'), may hold values from -384 to 384
- source_ids: int32 [8192], P('ctx'), may hold values from 0 to 63
- source_weights: float32 [64], replicated, may hold values from 0.25 to 4
- q_feature: float32 [4, 128, 128], P('head'), may hold values from -4 to 4
- k_feature: float32 [128, 128], replicated, may hold values from -4 to 4
Outputs:
- grad_queries: float32 [8192, 512], P('ctx', 'head')
- grad_keys: float32 [8192, 128], P(('ctx', 'head'))
- grad_values: float32 [8192, 128], P(('ctx', 'head'))
- grad_q_feature: float32 [4, 128, 128], P('head')
- grad_k_feature: float32 [128, 128], replicated
All inputs are finite; a program needn't handle non-finite values.
Results may differ from a plain program's by a relative error of at most 0.0015.
Values sent between devices are 32-bit elements; how exact they have to be, the bound alone decides.
No kernel may reach another device: no remote copies, remote signals or barrier semaphores. Data moves between devices by JAX's collectives and lax.ppermute only.
A program may use at most 64 MiB of HBM per device.

v0:
```python
import functools

import jax
import jax.numpy as jnp
from jax import lax
from jax.experimental import pallas as pl
from jax.experimental.pallas import tpu as pltpu
from jax.sharding import PartitionSpec as P


F32 = jnp.float32
BF16 = jnp.bfloat16
NN = ((1,), (0,))
NT = ((1,), (1,))
TN = ((0,), (0,))


def split(x):
    high = x.astype(BF16)
    return high, (x - high.astype(F32)).astype(BF16)


def joined(pair):
    return pair[0].astype(F32) + pair[1].astype(F32)


def raw_dot(a, b, dims):
    return lax.dot_general(a, b, (dims, ((), ())), preferred_element_type=F32)


def dot3(a, b, dims):
    return raw_dot(a[0], b[0], dims) + (raw_dot(a[0], b[1], dims) + raw_dot(a[1], b[0], dims))


def dot_exact(a, b, dims):
    return lax.dot_general(
        a, b, (dims, ((), ())), precision=lax.Precision.HIGHEST, preferred_element_type=F32
    )


def softmaxes(logits):
    upper = jnp.exp(logits - jnp.max(logits, axis=-1, keepdims=True))
    lower = jnp.exp(jnp.min(logits, axis=-1, keepdims=True) - logits)
    return (
        upper / jnp.sum(upper, axis=-1, keepdims=True),
        lower / jnp.sum(lower, axis=-1, keepdims=True),
    )


def logit_grad(features, grad):
    half = features.shape[1] // 2
    upper, lower = features[:, :half], features[:, half:]
    a, b = grad[:, :half], grad[:, half:]
    up = upper * (a - jnp.sum(upper * a, axis=-1, keepdims=True))
    return up - lower * (b - jnp.sum(lower * b, axis=-1, keepdims=True))


def digits_of(count):
    found, base = [], 1
    while base < count:
        radix = 4 if (count // base) % 4 == 0 else 2
        found.append((base, radix))
        base *= radix
    return found


def exchange(values, axis, base, radix):
    count = lax.axis_size(axis)
    received = []
    for m in range(1, radix):
        value = values[m - 1] if isinstance(values, (list, tuple)) else values
        received.append(
            lax.ppermute(value, axis, [(i, i ^ (base * m)) for i in range(count)])
        )
    return received


def grant(size):
    return (4 << 20) + 3 * size


def call(body, outs, args, flops=0, in_specs=None, out_specs=None, scratch=(), aliases=None):
    size = sum(4 * a.size for a in args) + sum(4 * o.size for o in outs)
    kwargs = {}
    if in_specs is not None:
        kwargs["in_specs"] = in_specs
    if out_specs is not None:
        kwargs["out_specs"] = out_specs
        kwargs["grid"] = (1,)
    return pl.pallas_call(
        body,
        out_shape=outs,
        scratch_shapes=scratch,
        input_output_aliases=aliases or {},
        cost_estimate=pl.CostEstimate(flops=flops, bytes_accessed=size, transcendentals=0),
        compiler_params=pltpu.CompilerParams(vmem_limit_bytes=grant(size)),
        **kwargs,
    )(*args)


def whole(shape):
    return pl.BlockSpec(shape, lambda i: (0,) * len(shape))


def out(shape, dtype=F32):
    return jax.ShapeDtypeStruct(shape, dtype)


def put_message(ref, state, totals):
    rows, half = state.shape[0], state.shape[1] // 2
    ref[0:rows] = state[:, :half]
    ref[rows : 2 * rows] = state[:, half:]
    first = lax.broadcasted_iota(jnp.int32, (8, half), 0) < 4
    ref[2 * rows : 2 * rows + 8] = jnp.where(first, totals[:, :half], totals[:, half:])


def take_totals(piece, rows):
    return jnp.concatenate(
        [piece[2 * rows : 2 * rows + 1], piece[2 * rows + 4 : 2 * rows + 5]], axis=1
    )


def put_state(piece, scratch, rows, owner):
    half = piece.shape[1]
    at = pl.ds(pl.multiple_of(owner * rows, 8), rows)
    scratch[at, :half] = piece[0:rows]
    scratch[at, half:] = piece[rows : 2 * rows]


def key_body(
    share, keys_hbm, values_hbm, weight_hbm, feat_high, feat_low, message,
    scratch, keys, values, weight, arrived,
):
    mine = lax.axis_index("head")
    pairs = [(keys_hbm, keys), (weight_hbm, weight), (values_hbm, values)]
    copies = [
        pltpu.make_async_copy(source, target, arrived.at[n])
        for n, (source, target) in enumerate(pairs)
    ]
    for copy in copies:
        copy.start()
    copies[0].wait()
    copies[1].wait()
    upper, lower = softmaxes(dot_exact(keys[...], weight[...], NN))
    feat = split(jnp.concatenate([upper, lower], axis=1))
    feat_high[...] = feat[0]
    feat_low[...] = feat[1]
    ones = jnp.ones((8, feat[0].shape[0]), BF16)
    totals = raw_dot(ones, feat[0], NN) + raw_dot(ones, feat[1], NN)
    copies[2].wait()
    scratch[...] = dot3(split(values[...]), feat, TN)
    state = scratch[pl.ds(pl.multiple_of(mine * share, 8), share), :]
    put_message(message, state, totals)


def causal(size):
    row = lax.broadcasted_iota(jnp.int32, (size, size), 0)
    col = lax.broadcasted_iota(jnp.int32, (size, size), 1)
    return row >= col


def query_body(
    block, queries, weight, values, key_high, key_low,
    feat_high, feat_low, score_high, score_low, numer, norm,
):
    upper, lower = softmaxes(dot_exact(queries[...], weight[0], NN))
    feat = split(jnp.concatenate([upper, lower], axis=1))
    feat_high[...] = feat[0]
    feat_low[...] = feat[1]
    rows, width = values.shape
    extended = split(jnp.concatenate([values[...], jnp.ones((rows, width), F32)], axis=1))
    mask = causal(block)
    for i in range(rows // block):
        at = slice(i * block, (i + 1) * block)
        total = None
        for j in range(i + 1):
            past = slice(j * block, (j + 1) * block)
            scores = dot3((feat[0][at], feat[1][at]), (key_high[past], key_low[past]), NT)
            if i == j:
                scores = jnp.where(mask, scores, 0.0)
            pair = split(scores)
            score_high[at, past] = pair[0]
            score_low[at, past] = pair[1]
            term = dot3(pair, (extended[0][past], extended[1][past]), NN)
            total = term if total is None else total + term
        numer[at] = total[:, :width]
        norm[at] = total[:, width:]


def scan_body(base, radix, local, *refs):
    received, (total, before) = refs[: radix - 1], refs[radix - 1 :]
    mine = (lax.axis_index("ctx") // base) % radix
    whole_sum, earlier = local[...], jnp.zeros(local.shape, F32)
    for m, piece in enumerate(received, 1):
        value = piece[...]
        whole_sum = whole_sum + value
        earlier = earlier + jnp.where((mine ^ m) < mine, value, 0.0)
    total[...] = whole_sum
    before[...] = earlier


def scan_last_body(base, radix, before, *refs):
    received, (result,) = refs[: radix - 1], refs[radix - 1 :]
    mine = (lax.axis_index("ctx") // base) % radix
    earlier = before[...]
    for m, piece in enumerate(received, 1):
        earlier = earlier + jnp.where((mine ^ m) < mine, piece[...], 0.0)
    result[...] = earlier


def inter_body(heads, peers, share, *refs):
    pieces, refs = refs[:peers], refs[peers:]
    feats, refs = [refs[2 * h : 2 * h + 2] for h in range(heads)], refs[2 * heads :]
    locals_, refs = [refs[2 * h : 2 * h + 2] for h in range(heads)], refs[2 * heads :]
    scaled, refs = refs[0], refs[1:]
    state_high, state_low = refs[:2]
    refs = refs[2:]
    grads, refs = refs[:heads], refs[heads:]
    messages, refs = refs[:peers], refs[peers:]
    scratch, = refs
    mine = lax.axis_index("head")
    for m, piece in enumerate(pieces):
        put_state(piece, scratch, share, mine ^ m)
    state = scratch[...]
    width = state.shape[0]
    totals = jnp.broadcast_to(take_totals(pieces[0], share), state.shape)
    extended = split(jnp.concatenate([state, totals], axis=0))
    state_high[...] = extended[0]
    state_low[...] = extended[1]
    carried = None
    for h in range(heads):
        feat = (feats[h][0][...], feats[h][1][...])
        inter = dot3(feat, extended, NT)
        numer = locals_[h][0][...] + inter[:, :width]
        norm = locals_[h][1][...] + inter[:, width:]
        mine_scaled = scaled[:, h * width : (h + 1) * width]
        grad_numer = mine_scaled / norm
        along = jnp.sum(mine_scaled * (numer / norm), axis=1, keepdims=True)
        both = jnp.concatenate([grad_numer, -(along / norm)], axis=1)
        grads[h][...] = both
        term = dot3(split(both), feat, TN)
        carried = term if carried is None else carried + term
    scratch[...] = carried[:width]
    for m, message in enumerate(messages):
        part = scratch[pl.ds(pl.multiple_of((mine ^ m) * share, 8), share), :]
        put_message(message, part, carried[width : width + 8])


def query_grad_body(
    block, first, queries, weight, values, key_high, key_low, feat_high, feat_low,
    score_high, score_low, grads, state_high, state_low, *refs,
):
    earlier, (grad_input, grad_weight, grad_key) = refs[1:-3], refs[-3:]
    rows, width = values.shape
    wide = key_high.shape[1]
    both = grads[...]
    numer = split(both[:, :width])
    scale = 1.0 / width
    extended = split(jnp.concatenate([both[:, :width], both[:, width:] * scale], axis=1))
    value_pair = split(values[...])
    feat = (feat_high[...], feat_low[...])
    state = (state_high[...], state_low[...])
    mask = causal(block)
    count = rows // block
    key_sums, value_sums, logit_parts = [None] * count, [None] * count, []
    cut = lambda pair, at: (pair[0][at], pair[1][at])
    for i in range(count):
        at = slice(i * block, (i + 1) * block)
        norm_part = both[at, width:]
        norm_part = jnp.concatenate([norm_part] * (block // width), axis=1)
        grad_query = dot3(cut(extended, at), state, NN)
        for j in range(i + 1):
            past = slice(j * block, (j + 1) * block)
            grad_scores = dot3(cut(numer, at), cut(value_pair, past), NT) + norm_part
            if i == j:
                grad_scores = jnp.where(mask, grad_scores, 0.0)
            pair = split(grad_scores)
            keys = (key_high[past], key_low[past])
            grad_query = grad_query + dot3(pair, keys, NN)
            key_term = dot3(pair, cut(feat, at), TN)
            value_term = dot3((score_high[at, past], score_low[at, past]), cut(numer, at), TN)
            key_sums[j] = key_term if key_sums[j] is None else key_sums[j] + key_term
            value_sums[j] = value_term if value_sums[j] is None else value_sums[j] + value_term
        logit_parts.append(logit_grad(joined(cut(feat, at)), grad_query))
    grad_logits = split(jnp.concatenate(logit_parts, axis=0))
    grad_input[...] = dot3(grad_logits, split(weight[0]), NT)
    grad_weight[...] = dot3(split(queries[...]), grad_logits, TN)
    for j in range(count):
        past = slice(j * block, (j + 1) * block)
        if first:
            grad_key[past, :wide] = key_sums[j]
            grad_key[past, wide:] = value_sums[j]
        else:
            grad_key[past, :wide] = earlier[0][past, :wide] + key_sums[j]
            grad_key[past, wide:] = earlier[0][past, wide:] + value_sums[j]


def sum_body(*refs):
    total = refs[0][...]
    for piece in refs[1:-1]:
        total = total + piece[...]
    refs[-1][...] = total


def suffix_weight_body(base, radix, above, heads, local, *refs):
    received, refs = refs[: above - 1], refs[above - 1 :]
    weights, (later, kept, *messages) = refs[:heads], refs[heads:]
    scratch = messages.pop()
    mine = (lax.axis_index("ctx") // base) % radix
    upper = (lax.axis_index("ctx") // (base * radix)) % above
    size = local.shape[0]
    width = weights[0].shape[0]
    shard = heads * width // radix
    for h, weight in enumerate(weights):
        scratch[h * width : (h + 1) * width] = weight[...]
    total = jnp.zeros(local.shape, F32)
    for m, piece in enumerate(received, 1):
        total = total + jnp.where((upper ^ m) > upper, piece[...], 0.0)
    later[...] = total
    rows = lambda m: pl.ds(pl.multiple_of((mine ^ m) * shard, 8), shard)
    kept[...] = scratch[rows(0), :]
    for m, message in enumerate(messages, 1):
        message[0:size] = total + jnp.where(mine > (mine ^ m), local[...], 0.0)
        message[size : size + shard] = scratch[rows(m), :]


def suffix_last_body(later, kept, *refs):
    received, (result, shard) = refs[:-2], refs[-2:]
    size = later.shape[0]
    total, sums = later[...], kept[...]
    for piece in received:
        total = total + piece[0:size]
        sums = sums + piece[size : size + sums.shape[0]]
    result[...] = total
    shard[...] = sums


def key_grad_body(share, piece, inner, values, keys, key_high, key_low, *refs):
    logit_ref, state_high, state_low, *parts, scratch, weights = refs
    mine = lax.axis_index("head")
    scratch[...] = jnp.zeros(scratch.shape, F32)
    put_state(piece, scratch, share, mine)
    state = split(scratch[...])
    state_high[...] = state[0]
    state_low[...] = state[1]
    totals = jnp.where(mine == 0, take_totals(piece, share), 0.0)
    wide = key_high.shape[1]
    grad = dot3(split(values[...]), state, NN) + totals + inner[:, :wide]
    feat = (key_high[...], key_low[...])
    grad_logits = logit_grad(joined(feat), grad)
    logit_ref[...] = grad_logits
    weights[...] = dot3(split(keys[...]), split(grad_logits), TN)
    rows = parts[0].shape[0]
    for m, target in enumerate(parts):
        target[...] = weights[pl.ds(pl.multiple_of((mine ^ m) * rows, 8), rows), :]


def key_out_body(part, logits, inner, state_high, state_low, weight, key_high, key_low, *refs):
    parts, both = refs[:-1], refs[-1]
    mine = lax.axis_index("head")
    width = weight.shape[0]
    wide = key_high.shape[1]
    feat = (key_high[...], key_low[...])
    both[:, :width] = dot3(split(logits[...]), split(weight[...]), NT)
    both[:, width:] = inner[:, wide:] + dot3(feat, (state_high[...], state_low[...]), NT)
    for m, target in enumerate(parts):
        target[...] = both[pl.ds(pl.multiple_of((mine ^ m) * part, 8), part), :]


def key_sum_body(*refs):
    pieces, (grad_key, grad_value) = refs[:-2], refs[-2:]
    total = pieces[0][...]
    for piece in pieces[1:]:
        total = total + piece[...]
    width = grad_key.shape[1]
    grad_key[...] = total[:, :width]
    grad_value[...] = total[:, width:]


def weight_message_body(*refs):
    parts, shard, message = refs[:-2], refs[-2], refs[-1]
    total = parts[0][...]
    for piece in parts[1:]:
        total = total + piece[...]
    rows = total.shape[0]
    message[0:rows] = total
    message[rows:] = shard[...]


def weight_last_body(base, radix, rows, local, *refs):
    received, (share, gathered) = refs[: radix - 1], refs[radix - 1 :]
    mine = (lax.axis_index("ctx") // base) % radix
    total = local[0:rows]
    shard = local.shape[0] - rows
    gathered[pl.ds(pl.multiple_of(mine * shard, 8), shard), :] = local[rows:]
    for m, piece in enumerate(received, 1):
        total = total + piece[0:rows]
        at = pl.ds(pl.multiple_of((mine ^ m) * shard, 8), shard)
        gathered[at, :] = piece[rows:]
    share[...] = total


def gather_body(rows, *refs):
    pieces, result = refs[:-1], refs[-1]
    mine = lax.axis_index("head")
    for m, piece in enumerate(pieces):
        result[pl.ds(pl.multiple_of((mine ^ m) * rows, 8), rows), :] = piece[...]


def backward(queries, keys, values, cotangent, source_ids, source_weights, q_feature, k_feature):
    heads, width, half = q_feature.shape
    wide = 2 * half
    rows = queries.shape[0]
    peers = lax.axis_size("head")
    share = width // peers
    part = rows // peers
    block = min(256, rows)
    digits = digits_of(lax.axis_size("ctx"))
    message = (2 * share + 8, half)
    bind = functools.partial
    unit = 2 * rows * width * wide
    hbm = pl.BlockSpec(memory_space=pltpu.HBM)

    source_index = lax.broadcasted_iota(jnp.int32, (1, source_weights.shape[0]), 1)
    lookup = source_ids[:, None] == source_index
    weight = jnp.sum(jnp.where(lookup, source_weights[None, :], 0.0), axis=1)
    scaled = cotangent * weight[:, None]

    feat_shape = out((rows, wide), BF16)
    key_high, key_low, local = call(
        bind(key_body, share),
        [feat_shape, feat_shape, out(message)],
        (keys, values, k_feature),
        6 * unit,
        [hbm] * 3,
        scratch=[
            pltpu.VMEM((width, wide), F32),
            pltpu.VMEM(keys.shape, F32),
            pltpu.VMEM(values.shape, F32),
            pltpu.VMEM(k_feature.shape, F32),
            pltpu.SemaphoreType.DMA((3,)),
        ],
    )

    before, total = None, local
    for place, (base, radix) in enumerate(digits):
        received = exchange(total, "ctx", base, radix)
        if place == 0:
            total, before = call(
                bind(scan_body, base, radix), [out(message)] * 2, (total, *received)
            )
        else:
            (before,) = call(bind(scan_last_body, base, radix), [out(message)], (before, *received))
            if place + 1 < len(digits):
                total = sum(received, total)
    prefix = [before] + exchange(before, "head", 1, peers)

    def head_specs(h):
        return [
            pl.BlockSpec((rows, width), lambda i: (0, h)),
            pl.BlockSpec((1, width, half), lambda i: (h, 0, 0)),
        ]

    feats, scores, inner = [], [], []
    for h in range(heads):
        args = (queries, q_feature, values, key_high, key_low)
        outs = (
            [feat_shape] * 2 + [out((rows, rows), BF16)] * 2 + [out((rows, width))] * 2
        )
        results = call(
            bind(query_body, block),
            outs,
            args,
            9 * unit,
            head_specs(h) + [whole(a.shape) for a in args[2:]],
            [whole(o.shape) for o in outs],
        )
        feats.append(results[0:2])
        scores.append(results[2:4])
        inner.append(results[4:6])

    results = call(
        bind(inter_body, heads, peers, share),
        [out((2 * width, wide), BF16)] * 2
        + [out((rows, 2 * width))] * heads
        + [out(message)] * peers,
        (
            *prefix,
            *[x for pair in feats for x in pair],
            *[x for pair in inner for x in pair],
            scaled,
        ),
        12 * heads * unit,
        scratch=[pltpu.VMEM((width, wide), F32)],
    )
    state, results = results[:2], results[2:]
    grads, results = results[:heads], results[heads:]
    sends = exchange(results[1:], "head", 1, peers)
    (carried,) = call(sum_body, [out(message)], (results[0], *sends))

    weight_grads = []
    grad_queries = key_inner = None
    for h in range(heads):
        args = [
            queries, q_feature, values, key_high, key_low, *feats[h], *scores[h], grads[h], *state,
        ]
        outs = [
            out((rows, heads * width)), out((width, half)), out((rows, wide + width)),
        ]
        specs = head_specs(h) + [whole(a.shape) for a in args[2:]]
        aliases = {}
        if h > 0:
            aliases = {len(args): 0}
            args += [grad_queries, key_inner]
            specs += [pl.BlockSpec(memory_space=pl.ANY), whole(key_inner.shape)]
        grad_queries, grad_weight, key_inner = call(
            bind(query_grad_body, block, h == 0),
            outs,
            args,
            15 * unit,
            specs,
            [head_specs(h)[0]] + [whole(o.shape) for o in outs[1:]],
            aliases=aliases,
        )
        weight_grads.append(grad_weight)

    later, messages = None, carried
    base_low, radix_low = digits[0]
    shard = heads * width // radix_low
    for place in range(len(digits) - 1, 0, -1):
        base, radix = digits[place]
        received = exchange(messages, "ctx", base, radix)
        below_base, below_radix = digits[place - 1]
        if place == 1 and len(digits) == 2:
            results = call(
                bind(suffix_weight_body, base_low, radix_low, radix, heads),
                [out(message), out((shard, half))]
                + [out((message[0] + shard, half))] * (radix_low - 1),
                (carried, *received, *weight_grads),
                scratch=[pltpu.VMEM((heads * width, half), F32)],
            )
            later, kept, messages = results[0], results[1], results[2:]
        else:
            mine = (lax.axis_index("ctx") // base) % radix
            if place == len(digits) - 1:
                later = sum(jnp.where((mine ^ m) > mine, r, 0.0) for m, r in enumerate(received, 1))
            else:
                later = sum(received, later)
            below = (lax.axis_index("ctx") // below_base) % below_radix
            messages = [
                later + jnp.where(below > (below ^ m), carried, 0.0) for m in range(1, below_radix)
            ]
            if place == 1:
                stacked = jnp.concatenate(weight_grads, axis=0)
                cut = lambda m: lax.dynamic_slice_in_dim(stacked, (below ^ m) * shard, shard, 0)
                kept = cut(0)
                messages = [
                    jnp.concatenate([part_message, cut(m)], axis=0)
                    for m, part_message in enumerate(messages, 1)
                ]
    received = exchange(messages, "ctx", base_low, radix_low)
    later, q_shard = call(
        suffix_last_body, [out(message), out((shard, half))], (later, kept, *received)
    )

    weight_rows = width // peers
    results = call(
        bind(key_grad_body, share),
        [out((rows, half))]
        + [out((width, wide), BF16)] * 2
        + [out((weight_rows, half))] * peers,
        (later, key_inner, values, keys, key_high, key_low),
        6 * unit,
        scratch=[pltpu.VMEM((width, wide), F32), pltpu.VMEM((width, half), F32)],
    )
    key_logits, later_high, later_low = results[:3]
    weight_parts = results[3:]
    weight_parts = [weight_parts[0]] + exchange(weight_parts[1:], "head", 1, peers)
    (total,) = call(
        weight_message_body, [out((weight_rows + shard, half))], (*weight_parts, q_shard)
    )
    key_parts = call(
        bind(key_out_body, part),
        [out((part, 2 * width))] * peers,
        (key_logits, key_inner, later_high, later_low, k_feature, key_high, key_low),
        6 * unit,
        scratch=[pltpu.VMEM((rows, 2 * width), F32)],
    )
    key_parts = [key_parts[0]] + exchange(key_parts[1:], "head", 1, peers)
    grad_keys, grad_values = call(key_sum_body, [out((part, width))] * 2, key_parts)
    for place in range(len(digits) - 1, 0, -1):
        base, radix = digits[place]
        received = exchange(total, "ctx", base, radix)
        (total,) = call(sum_body, [out(total.shape)], (total, *received))
    received = exchange(total, "ctx", base_low, radix_low)
    k_share, q_sum = call(
        bind(weight_last_body, base_low, radix_low, weight_rows),
        [out((weight_rows, half)), out((heads * width, half))],
        (total, *received),
    )
    shares = [k_share] + exchange(k_share, "head", 1, peers)
    (k_sum,) = call(bind(gather_body, weight_rows), [out((width, half))], shares)
    return (
        grad_queries,
        grad_keys,
        grad_values,
        q_sum.reshape(heads, width, half),
        k_sum,
    )


def solution(mesh):
    placed = (
        P("ctx", "head"),
        P("ctx", None),
        P("ctx", None),
        P("ctx", "head"),
        P("ctx"),
        P(),
        P("head", None, None),
        P(),
    )
    return jax.shard_map(
        backward,
        mesh=mesh,
        in_specs=placed,
        out_specs=(
            P("ctx", "head"),
            P(("ctx", "head"), None),
            P(("ctx", "head"), None),
            P("head", None, None),
            P(),
        ),
        check_vma=False,
    )
```

profile of v0, /device:TPU:0, one launch (start us, length us, event | category | flops | bytes accessed | tf_op | source)
XLA Modules:
  0.0 70.4 jit_solution(9779266249810166128)
XLA Ops:
  3.4 1.5 %shard_map.119 = (bf16[512,256]{1,0:T(8,128)(2,1)S(1)}, bf16[512,256]{1,0:T(8,128)(2,1)S(1)}, f32[136,128]{1,0:T(8,128)S(1)}) custom-call(f32[512,128]{1,0:T(8,128)S(1)} %copy-done.4, f32[512,128]{1,0:T(8,128)S(1)} %copy-done.1, f32[128,128]{1,0:T(8,128)S(1)} %copy-done.6), custom_call_target="tpu_custom_call" | custom-call | flops 201326592 | bytes 1708032 | tf_op jit(solution)/shard_map/pallas_call | solution.py:90
  4.9 4.0 %collective-permute-start.2 = (f32[136,128]{1,0:T(8,128)S(1)}, f32[136,128]{1,0:T(8,128)S(1)}, u32[]{:S(2)}, u32[]{:S(2)}) collective-permute-start(f32[136,128]{1,0:T(8,128)S(1)} %get-tuple-element.58.local), channel_id=1, source_target_pairs={{0,6},{2,4},{4,2},{6,0},{8,14},{10,12},{12,10},{14,8},{16,22},{18,... | collective-permute-start | bytes 208904 | tf_op jit(solution)/shard_map/ppermute | solution.py:73
  9.5 1.7 %collective-permute-done.2.refs_2_ = f32[136,128]{1,0:T(8,128)S(1)} collective-permute-done((f32[136,128]{1,0:T(8,128)S(1)}, f32[136,128]{1,0:T(8,128)S(1)}, u32[]{:S(2)}, u32[]{:S(2)}) %collective-permute-start.2) | collective-permute-done | bytes 69664 | tf_op jit(solution)/shard_map/ppermute | solution.py:73
  11.2 2.0 %collective-permute-done.1.refs_1_ = f32[136,128]{1,0:T(8,128)S(1)} collective-permute-done((f32[136,128]{1,0:T(8,128)S(1)}, f32[136,128]{1,0:T(8,128)S(1)}, u32[]{:S(2)}, u32[]{:S(2)}) %collective-permute-start.1) | collective-permute-done | bytes 69664 | tf_op jit(solution)/shard_map/ppermute | solution.py:73
  13.8 3.7 %collective-permute-start.5 = (f32[136,128]{1,0:T(8,128)S(1)}, f32[136,128]{1,0:T(8,128)S(1)}, u32[]{:S(2)}, u32[]{:S(2)}) collective-permute-start(f32[136,128]{1,0:T(8,128)S(1)} %get-tuple-element.60), channel_id=1, source_target_pairs={{0,24},{2,26},{4,28},{6,30},{8,16},{10,18},{12,20},{14,22},{16,8},... | collective-permute-start | bytes 208904 | tf_op jit(solution)/shard_map/ppermute | solution.py:73
  18.3 1.7 %collective-permute-done.5.refs_2_ = f32[136,128]{1,0:T(8,128)S(1)} collective-permute-done((f32[136,128]{1,0:T(8,128)S(1)}, f32[136,128]{1,0:T(8,128)S(1)}, u32[]{:S(2)}, u32[]{:S(2)}) %collective-permute-start.5) | collective-permute-done | bytes 69664 | tf_op jit(solution)/shard_map/ppermute | solution.py:73
  20.0 2.8 %collective-permute-done.4.refs_1_ = f32[136,128]{1,0:T(8,128)S(1)} collective-permute-done((f32[136,128]{1,0:T(8,128)S(1)}, f32[136,128]{1,0:T(8,128)S(1)}, u32[]{:S(2)}, u32[]{:S(2)}) %collective-permute-start.4) | collective-permute-done | bytes 69664 | tf_op jit(solution)/shard_map/ppermute | solution.py:73
  24.0 1.6 %shard_map.123 = (bf16[512,256]{1,0:T(8,128)(2,1)S(1)}, bf16[512,256]{1,0:T(8,128)(2,1)S(1)}, bf16[512,512]{1,0:T(8,128)(2,1)S(1)}, bf16[512,512]{1,0:T(8,128)(2...) custom-call(f32[512,256]{1,0:T(8,128)S(1)} %copy-done, f32[2,128,128]{2,1,0:T(8,128)S(1)} %copy-done.3, ...), custom_call_target="tpu_custom_call" | custom-call | flops 301989888 | bytes 5636096 | tf_op jit(solution)/shard_map/pallas_call | solution.py:90
  25.7 1.6 %shard_map.120 = (bf16[512,256]{1,0:T(8,128)(2,1)S(1)}, bf16[512,256]{1,0:T(8,128)(2,1)S(1)}, bf16[512,512]{1,0:T(8,128)(2,1)S(1)}, bf16[512,512]{1,0:T(8,128)(2...) custom-call(f32[512,256]{1,0:T(8,128)S(1)} %copy-done, f32[2,128,128]{2,1,0:T(8,128)S(1)} %copy-done.3, ...), custom_call_target="tpu_custom_call" | custom-call | flops 301989888 | bytes 5636096 | tf_op jit(solution)/shard_map/pallas_call | solution.py:90
  27.3 1.6 %shard_map.124 = (bf16[256,256]{1,0:T(8,128)(2,1)S(1)}, bf16[256,256]{1,0:T(8,128)(2,1)S(1)}, f32[512,256]{1,0:T(8,128)S(1)}, f32[512,256]{1,0:T(8,128)S(1)}, f3...) custom-call(f32[136,128]{1,0:T(8,128)S(1)} %shard_map.122.refs_0_, f32[136,128]{1,0:T(8,128)S(1)} %collective-permute-done.6.refs_1_, ...), custom_call_target="tpu_custom_call" | custom-call | flops 805306368 | bytes 5521408 | tf_op jit(solution)/shard_map/pallas_call | solution.py:90
  29.0 1.2 %collective-permute-done.7.refs_1_ = f32[136,128]{1,0:T(8,128)S(1)} collective-permute-done((f32[136,128]{1,0:T(8,128)S(1)}, f32[136,128]{1,0:T(8,128)S(1)}, u32[]{:S(2)}, u32[]{:S(2)}) %collective-permute-start.7) | collective-permute-done | bytes 69664 | tf_op jit(solution)/shard_map/ppermute | solution.py:73
  30.2 2.3 %collective-permute-start.10 = (f32[136,128]{1,0:T(8,128)S(1)}, f32[136,128]{1,0:T(8,128)S(1)}, u32[]{:S(2)}, u32[]{:S(2)}) collective-permute-start(f32[136,128]{1,0:T(8,128)S(1)} %shard_map.127.local), channel_id=1, source_target_pairs={{0,24},{2,26},{4,28},{6,30},{8,16},{10,18},{12,20},{14,22},{16,8},... | collective-permute-start | bytes 208904 | tf_op jit(solution)/shard_map/ppermute | solution.py:73
  32.6 2.1 %collective-permute-start.8 = (f32[136,128]{1,0:T(8,128)S(1)}, f32[136,128]{1,0:T(8,128)S(1)}, u32[]{:S(2)}, u32[]{:S(2)}) collective-permute-start(f32[136,128]{1,0:T(8,128)S(1)} %shard_map.127.local), channel_id=1, source_target_pairs={{0,8},{2,10},{4,12},{6,14},{8,0},{10,2},{12,4},{14,6},{16,24},{18,... | collective-permute-start | bytes 208904 | tf_op jit(solution)/shard_map/ppermute | solution.py:73
  34.7 2.8 %shard_map.125 = (f32[512,256]{1,0:T(8,128)}, f32[128,128]{1,0:T(8,128)S(1)}, f32[512,384]{1,0:T(8,128)S(1)}) custom-call(f32[512,256]{1,0:T(8,128)S(1)} %copy-done, f32[2,128,128]{2,1,0:T(8,128)S(1)} %copy-done.3, f32[512,128]{1,0:T(8,128)S(1)} %copy-done.2, bf16[512,256]{1,0:T(8,128)(2,1)S(1)} %get-tuple-element.52.key_high, ...), custom_call_target="tpu_custom_call" | custom-call | flops 503316480 | bytes 7536640 | tf_op jit(solution)/shard_map/pallas_call | solution.py:90
  37.5 2.7 %shard_map.126 = (f32[512,256]{1,0:T(8,128)}, f32[128,128]{1,0:T(8,128)S(1)}, f32[512,384]{1,0:T(8,128)S(1)}) custom-call(f32[512,256]{1,0:T(8,128)S(1)} %copy-done, f32[2,128,128]{2,1,0:T(8,128)S(1)} %copy-done.3, f32[512,128]{1,0:T(8,128)S(1)} %copy-done.2, bf16[512,256]{1,0:T(8,128)(2,1)S(1)} %get-tuple-element.52.key_high, ...), custom_call_target="tpu_custom_call", output_to_operand_aliasing={{0}: (12, {})} | custom-call | flops 503316480 | bytes 8847360 | tf_op jit(solution)/shard_map/pallas_call | solution.py:90
  42.4 1.4 %collective-permute-start.13 = (f32[200,128]{1,0:T(8,128)S(1)}, f32[200,128]{1,0:T(8,128)S(1)}, u32[]{:S(2)}, u32[]{:S(2)}) collective-permute-start(f32[200,128]{1,0:T(8,128)S(1)} %get-tuple-element.84), channel_id=1, source_target_pairs={{0,6},{2,4},{4,2},{6,0},{8,14},{10,12},{12,10},{14,8},{16,22},{18,... | collective-permute-start | bytes 307208 | tf_op jit(solution)/shard_map/ppermute | solution.py:73
  43.8 2.1 %collective-permute-done.11.refs_0_ = f32[200,128]{1,0:T(8,128)S(1)} collective-permute-done((f32[200,128]{1,0:T(8,128)S(1)}, f32[200,128]{1,0:T(8,128)S(1)}, u32[]{:S(2)}, u32[]{:S(2)}) %collective-permute-start.11) | collective-permute-done | bytes 102432 | tf_op jit(solution)/shard_map/ppermute | solution.py:73
  51.1 2.5 %collective-permute-start.18 = (f32[128,128]{1,0:T(8,128)S(1)}, f32[128,128]{1,0:T(8,128)S(1)}, u32[]{:S(2)}, u32[]{:S(2)}) collective-permute-start(f32[128,128]{1,0:T(8,128)S(1)} %shard_map.133.refs_0_), channel_id=1, source_target_pairs={{0,24},{2,26},{4,28},{6,30},{8,16},{10,18},{12,20},{14,22},{16,8},... | collective-permute-start | bytes 196616 | tf_op jit(solution)/shard_map/ppermute | solution.py:73
  53.6 1.9 %collective-permute-start.16 = (f32[128,128]{1,0:T(8,128)S(1)}, f32[128,128]{1,0:T(8,128)S(1)}, u32[]{:S(2)}, u32[]{:S(2)}) collective-permute-start(f32[128,128]{1,0:T(8,128)S(1)} %shard_map.133.refs_0_), channel_id=1, source_target_pairs={{0,8},{2,10},{4,12},{6,14},{8,0},{10,2},{12,4},{14,6},{16,24},{18,... | collective-permute-start | bytes 196616 | tf_op jit(solution)/shard_map/ppermute | solution.py:73
  55.5 2.3 %collective-permute-done.18.refs_3_ = f32[128,128]{1,0:T(8,128)S(1)} collective-permute-done((f32[128,128]{1,0:T(8,128)S(1)}, f32[128,128]{1,0:T(8,128)S(1)}, u32[]{:S(2)}, u32[]{:S(2)}) %collective-permute-start.18) | collective-permute-done | bytes 65568 | tf_op jit(solution)/shard_map/ppermute | solution.py:73
  57.9 2.0 %collective-permute-done.17.refs_2_ = f32[128,128]{1,0:T(8,128)S(1)} collective-permute-done((f32[128,128]{1,0:T(8,128)S(1)}, f32[128,128]{1,0:T(8,128)S(1)}, u32[]{:S(2)}, u32[]{:S(2)}) %collective-permute-start.17) | collective-permute-done | bytes 65568 | tf_op jit(solution)/shard_map/ppermute | solution.py:73
  59.9 1.8 %collective-permute-start.21 = (f32[128,128]{1,0:T(8,128)S(1)}, f32[128,128]{1,0:T(8,128)S(1)}, u32[]{:S(2)}, u32[]{:S(2)}) collective-permute-start(f32[128,128]{1,0:T(8,128)S(1)} %shard_map.134.local), channel_id=1, source_target_pairs={{0,6},{2,4},{4,2},{6,0},{8,14},{10,12},{12,10},{14,8},{16,22},{18,... | collective-permute-start | bytes 196616 | tf_op jit(solution)/shard_map/ppermute | solution.py:73
  63.5 1.7 %collective-permute-done.21.refs_2_ = f32[128,128]{1,0:T(8,128)S(1)} collective-permute-done((f32[128,128]{1,0:T(8,128)S(1)}, f32[128,128]{1,0:T(8,128)S(1)}, u32[]{:S(2)}, u32[]{:S(2)}) %collective-permute-start.21) | collective-permute-done | bytes 65568 | tf_op jit(solution)/shard_map/ppermute | solution.py:73
  67.8 1.2 %collective-permute-done.22.refs_1_ = f32[64,128]{1,0:T(8,128)S(1)} collective-permute-done((f32[64,128]{1,0:T(8,128)S(1)}, f32[64,128]{1,0:T(8,128)S(1)}, u32[]{:S(2)}, u32[]{:S(2)}) %collective-permute-start.22) | collective-permute-done | bytes 32800 | tf_op jit(solution)/shard_map/ppermute | solution.py:73
  (64 shorter events, 19.1 us)
Async XLA Ops:
  3.4 19.6 %copy-start.8 = (f32[512,256]{1,0:T(8,128)S(1)}, f32[512,256]{1,0:T(8,128)}, u32[]{:S(2)}) copy-start(f32[512,256]{1,0:T(8,128)} %param.11) | copy-start | bytes 1572868
  4.9 6.3 %collective-permute-start.2 = (f32[136,128]{1,0:T(8,128)S(1)}, f32[136,128]{1,0:T(8,128)S(1)}, u32[]{:S(2)}, u32[]{:S(2)}) collective-permute-start(f32[136,128]{1,0:T(8,128)S(1)} %get-tuple-element.58.local), channel_id=1, source_target_pairs={{0,6},{2,4},{4,2},{6,0},{8,14},{10,12},{12,10},{14,8},{16,22},{18,... | collective-permute-start | bytes 208904 | tf_op jit(solution)/shard_map/ppermute | solution.py:73
  8.9 4.3 %collective-permute-start.1 = (f32[136,128]{1,0:T(8,128)S(1)}, f32[136,128]{1,0:T(8,128)S(1)}, u32[]{:S(2)}, u32[]{:S(2)}) collective-permute-start(f32[136,128]{1,0:T(8,128)S(1)} %get-tuple-element.58.local), channel_id=1, source_target_pairs={{0,4},{2,6},{4,0},{6,2},{8,12},{10,14},{12,8},{14,10},{16,20},{18,... | collective-permute-start | bytes 208904 | tf_op jit(solution)/shard_map/ppermute | solution.py:73
  9.4 4.3 %collective-permute-start = (f32[136,128]{1,0:T(8,128)S(1)}, f32[136,128]{1,0:T(8,128)S(1)}, u32[]{:S(2)}, u32[]{:S(2)}) collective-permute-start(f32[136,128]{1,0:T(8,128)S(1)} %get-tuple-element.58.local), channel_id=1, source_target_pairs={{0,2},{2,0},{4,6},{6,4},{8,10},{10,8},{12,14},{14,12},{16,18},{18,... | collective-permute-start | bytes 208904 | tf_op jit(solution)/shard_map/ppermute | solution.py:73
  13.8 6.3 %collective-permute-start.5 = (f32[136,128]{1,0:T(8,128)S(1)}, f32[136,128]{1,0:T(8,128)S(1)}, u32[]{:S(2)}, u32[]{:S(2)}) collective-permute-start(f32[136,128]{1,0:T(8,128)S(1)} %get-tuple-element.60), channel_id=1, source_target_pairs={{0,24},{2,26},{4,28},{6,30},{8,16},{10,18},{12,20},{14,22},{16,8},... | collective-permute-start | bytes 208904 | tf_op jit(solution)/shard_map/ppermute | solution.py:73
  17.4 5.4 %collective-permute-start.4 = (f32[136,128]{1,0:T(8,128)S(1)}, f32[136,128]{1,0:T(8,128)S(1)}, u32[]{:S(2)}, u32[]{:S(2)}) collective-permute-start(f32[136,128]{1,0:T(8,128)S(1)} %get-tuple-element.60), channel_id=1, source_target_pairs={{0,16},{2,18},{4,20},{6,22},{8,24},{10,26},{12,28},{14,30},{16,0},... | collective-permute-start | bytes 208904 | tf_op jit(solution)/shard_map/ppermute | solution.py:73
  17.4 5.4 %collective-permute-start.3 = (f32[136,128]{1,0:T(8,128)S(1)}, f32[136,128]{1,0:T(8,128)S(1)}, u32[]{:S(2)}, u32[]{:S(2)}) collective-permute-start(f32[136,128]{1,0:T(8,128)S(1)} %get-tuple-element.60), channel_id=1, source_target_pairs={{0,8},{2,10},{4,12},{6,14},{8,0},{10,2},{12,4},{14,6},{16,24},{18,... | collective-permute-start | bytes 208904 | tf_op jit(solution)/shard_map/ppermute | solution.py:73
  22.9 4.3 %collective-permute-start.6 = (f32[136,128]{1,0:T(8,128)S(1)}, f32[136,128]{1,0:T(8,128)S(1)}, u32[]{:S(2)}, u32[]{:S(2)}) collective-permute-start(f32[136,128]{1,0:T(8,128)S(1)} %shard_map.122.refs_0_), channel_id=1, source_target_pairs={{0,1},{1,0},{2,3},{3,2},{4,5},{5,4},{6,7},{7,6},{8,9},{9,8},{10,11... | collective-permute-start | bytes 208904 | tf_op jit(solution)/shard_map/ppermute | solution.py:73
  28.9 1.3 %collective-permute-start.7 = (f32[136,128]{1,0:T(8,128)S(1)}, f32[136,128]{1,0:T(8,128)S(1)}, u32[]{:S(2)}, u32[]{:S(2)}) collective-permute-start(f32[136,128]{1,0:T(8,128)S(1)} %get-tuple-element.77), channel_id=1, source_target_pairs={{0,1},{1,0},{2,3},{3,2},{4,5},{5,4},{6,7},{7,6},{8,9},{9,8},{10,11... | collective-permute-start | bytes 208904 | tf_op jit(solution)/shard_map/ppermute | solution.py:73
  30.2 10.0 %collective-permute-start.10 = (f32[136,128]{1,0:T(8,128)S(1)}, f32[136,128]{1,0:T(8,128)S(1)}, u32[]{:S(2)}, u32[]{:S(2)}) collective-permute-start(f32[136,128]{1,0:T(8,128)S(1)} %shard_map.127.local), channel_id=1, source_target_pairs={{0,24},{2,26},{4,28},{6,30},{8,16},{10,18},{12,20},{14,22},{16,8},... | collective-permute-start | bytes 208904 | tf_op jit(solution)/shard_map/ppermute | solution.py:73
  32.6 7.6 %collective-permute-start.9 = (f32[136,128]{1,0:T(8,128)S(1)}, f32[136,128]{1,0:T(8,128)S(1)}, u32[]{:S(2)}, u32[]{:S(2)}) collective-permute-start(f32[136,128]{1,0:T(8,128)S(1)} %shard_map.127.local), channel_id=1, source_target_pairs={{0,16},{2,18},{4,20},{6,22},{8,24},{10,26},{12,28},{14,30},{16,0},... | collective-permute-start | bytes 208904 | tf_op jit(solution)/shard_map/ppermute | solution.py:73
  32.6 7.6 %collective-permute-start.8 = (f32[136,128]{1,0:T(8,128)S(1)}, f32[136,128]{1,0:T(8,128)S(1)}, u32[]{:S(2)}, u32[]{:S(2)}) collective-permute-start(f32[136,128]{1,0:T(8,128)S(1)} %shard_map.127.local), channel_id=1, source_target_pairs={{0,8},{2,10},{4,12},{6,14},{8,0},{10,2},{12,4},{14,6},{16,24},{18,... | collective-permute-start | bytes 208904 | tf_op jit(solution)/shard_map/ppermute | solution.py:73
  40.3 5.6 %collective-permute-start.11 = (f32[200,128]{1,0:T(8,128)S(1)}, f32[200,128]{1,0:T(8,128)S(1)}, u32[]{:S(2)}, u32[]{:S(2)}) collective-permute-start(f32[200,128]{1,0:T(8,128)S(1)} %get-tuple-element.82), channel_id=1, source_target_pairs={{0,2},{2,0},{4,6},{6,4},{8,10},{10,8},{12,14},{14,12},{16,18},{18,... | collective-permute-start | bytes 307208 | tf_op jit(solution)/shard_map/ppermute | solution.py:73
  41.3 5.6 %collective-permute-start.12 = (f32[200,128]{1,0:T(8,128)S(1)}, f32[200,128]{1,0:T(8,128)S(1)}, u32[]{:S(2)}, u32[]{:S(2)}) collective-permute-start(f32[200,128]{1,0:T(8,128)S(1)} %get-tuple-element.83), channel_id=1, source_target_pairs={{0,4},{2,6},{4,0},{6,2},{8,12},{10,14},{12,8},{14,10},{16,20},{18,... | collective-permute-start | bytes 307208 | tf_op jit(solution)/shard_map/ppermute | solution.py:73
  42.4 5.6 %collective-permute-start.13 = (f32[200,128]{1,0:T(8,128)S(1)}, f32[200,128]{1,0:T(8,128)S(1)}, u32[]{:S(2)}, u32[]{:S(2)}) collective-permute-start(f32[200,128]{1,0:T(8,128)S(1)} %get-tuple-element.84), channel_id=1, source_target_pairs={{0,6},{2,4},{4,2},{6,0},{8,14},{10,12},{12,10},{14,8},{16,22},{18,... | collective-permute-start | bytes 307208 | tf_op jit(solution)/shard_map/ppermute | solution.py:73
  49.4 20.2 %collective-permute-start.14 = (f32[256,256]{1,0:T(8,128)S(1)}, f32[256,256]{1,0:T(8,128)S(1)}, u32[]{:S(2)}, u32[]{:S(2)}) collective-permute-start(f32[256,256]{1,0:T(8,128)S(1)} %get-tuple-element.91), channel_id=1, source_target_pairs={{0,1},{1,0},{2,3},{3,2},{4,5},{5,4},{6,7},{7,6},{8,9},{9,8},{10,11... | collective-permute-start | bytes 786440 | tf_op jit(solution)/shard_map/ppermute | solution.py:73
  49.5 1.6 %collective-permute-start.15 = (f32[64,128]{1,0:T(8,128)S(1)}, f32[64,128]{1,0:T(8,128)S(1)}, u32[]{:S(2)}, u32[]{:S(2)}) collective-permute-start(f32[64,128]{1,0:T(8,128)S(1)} %get-tuple-element.95), channel_id=1, source_target_pairs={{0,1},{1,0},{2,3},{3,2},{4,5},{5,4},{6,7},{7,6},{8,9},{9,8},{10,11... | collective-permute-start | bytes 98312 | tf_op jit(solution)/shard_map/ppermute | solution.py:73
  51.1 6.8 %collective-permute-start.18 = (f32[128,128]{1,0:T(8,128)S(1)}, f32[128,128]{1,0:T(8,128)S(1)}, u32[]{:S(2)}, u32[]{:S(2)}) collective-permute-start(f32[128,128]{1,0:T(8,128)S(1)} %shard_map.133.refs_0_), channel_id=1, source_target_pairs={{0,24},{2,26},{4,28},{6,30},{8,16},{10,18},{12,20},{14,22},{16,8},... | collective-permute-start | bytes 196616 | tf_op jit(solution)/shard_map/ppermute | solution.py:73
  53.6 6.3 %collective-permute-start.17 = (f32[128,128]{1,0:T(8,128)S(1)}, f32[128,128]{1,0:T(8,128)S(1)}, u32[]{:S(2)}, u32[]{:S(2)}) collective-permute-start(f32[128,128]{1,0:T(8,128)S(1)} %shard_map.133.refs_0_), channel_id=1, source_target_pairs={{0,16},{2,18},{4,20},{6,22},{8,24},{10,26},{12,28},{14,30},{16,0},... | collective-permute-start | bytes 196616 | tf_op jit(solution)/shard_map/ppermute | solution.py:73
  53.6 6.3 %collective-permute-start.16 = (f32[128,128]{1,0:T(8,128)S(1)}, f32[128,128]{1,0:T(8,128)S(1)}, u32[]{:S(2)}, u32[]{:S(2)}) collective-permute-start(f32[128,128]{1,0:T(8,128)S(1)} %shard_map.133.refs_0_), channel_id=1, source_target_pairs={{0,8},{2,10},{4,12},{6,14},{8,0},{10,2},{12,4},{14,6},{16,24},{18,... | collective-permute-start | bytes 196616 | tf_op jit(solution)/shard_map/ppermute | solution.py:73
  59.9 5.2 %collective-permute-start.21 = (f32[128,128]{1,0:T(8,128)S(1)}, f32[128,128]{1,0:T(8,128)S(1)}, u32[]{:S(2)}, u32[]{:S(2)}) collective-permute-start(f32[128,128]{1,0:T(8,128)S(1)} %shard_map.134.local), channel_id=1, source_target_pairs={{0,6},{2,4},{4,2},{6,0},{8,14},{10,12},{12,10},{14,8},{16,22},{18,... | collective-permute-start | bytes 196616 | tf_op jit(solution)/shard_map/ppermute | solution.py:73
  61.8 4.5 %collective-permute-start.20 = (f32[128,128]{1,0:T(8,128)S(1)}, f32[128,128]{1,0:T(8,128)S(1)}, u32[]{:S(2)}, u32[]{:S(2)}) collective-permute-start(f32[128,128]{1,0:T(8,128)S(1)} %shard_map.134.local), channel_id=1, source_target_pairs={{0,4},{2,6},{4,0},{6,2},{8,12},{10,14},{12,8},{14,10},{16,20},{18,... | collective-permute-start | bytes 196616 | tf_op jit(solution)/shard_map/ppermute | solution.py:73
  62.8 4.3 %collective-permute-start.19 = (f32[128,128]{1,0:T(8,128)S(1)}, f32[128,128]{1,0:T(8,128)S(1)}, u32[]{:S(2)}, u32[]{:S(2)}) collective-permute-start(f32[128,128]{1,0:T(8,128)S(1)} %shard_map.134.local), channel_id=1, source_target_pairs={{0,2},{2,0},{4,6},{6,4},{8,10},{10,8},{12,14},{14,12},{16,18},{18,... | collective-permute-start | bytes 196616 | tf_op jit(solution)/shard_map/ppermute | solution.py:73
  67.8 1.2 %collective-permute-start.22 = (f32[64,128]{1,0:T(8,128)S(1)}, f32[64,128]{1,0:T(8,128)S(1)}, u32[]{:S(2)}, u32[]{:S(2)}) collective-permute-start(f32[64,128]{1,0:T(8,128)S(1)} %get-tuple-element.98.refs_0_), channel_id=1, source_target_pairs={{0,1},{1,0},{2,3},{3,2},{4,5},{5,4},{6,7},{7,6},{8,9},{9,8},{10,11... | collective-permute-start | bytes 98312 | tf_op jit(solution)/shard_map/ppermute | solution.py:73
  (10 other events, 23.6 us)
where the time goes:
time: 70.6 us; the launch traced here: 70.4 us
  starting transfers between devices  25.8 us (37%)
  waiting for transfers between devices  24.4 us (35%)
  Pallas kernels  15.5 us (22%)
  local copies, waits for them, and re-layouts  3.65 us (5%)
  between operations  0.84 us (1%)
    ppermute x23, starting transfers between devices, exchange(): lax.ppermute(value, axis, [(i, i ^ base * m) for i in range(count)])  25.8 us
    ppermute x23, waiting for transfers between devices, exchange(): lax.ppermute(value, axis, [(i, i ^ base * m) for i in range(count)])  24.4 us
    pallas_call x18, Pallas kernels, call(): pl.pallas_call(body, out_shape=outs, scratch_shapes=scratch, input_output...  15.5 us
    unnamed x22, local copies, waits for them, and re-layouts  3.65 us
  transfers between devices with their start and end apart: 23, of which 16 were waited for; matrix products, arithmetic and copies ran while one was open for 0% of the time, Pallas kernels for 14%

commit v1 on v0

--- a/solution.py
+++ b/solution.py
@@ -64,14 +64,47 @@
     return found
 
 
-def exchange(values, axis, base, radix):
-    count = lax.axis_size(axis)
+def rounds_of(count, peers, rising):
+    digits = digits_of(count)
+    radices = [radix for _, radix in digits]
+    joint = peers % 2 == 0 and radices == radices[::-1]
+    even = digits if rising else digits[::-1]
+    odd = even[::-1] if joint else even
+    ups = (rising, (not rising) if joint else rising)
+    return [(e[0], o[0], e[1]) for e, o in zip(even, odd)], ups
+
+
+def position(step):
+    even, odd, radix = step
+    index = lax.axis_index("ctx")
+    is_odd = lax.axis_index("head") % 2 == 1
+    return jnp.where(is_odd, (index // odd) % radix, (index // even) % radix)
+
+
+def is_up(ups):
+    return (lax.axis_index("head") % 2 == 1) == ups[1] if ups[0] != ups[1] else ups[0]
+
+
+def swap(values, step):
+    even, odd, radix = step
+    count, peers = lax.axis_size("ctx"), lax.axis_size("head")
     received = []
     for m in range(1, radix):
         value = values[m - 1] if isinstance(values, (list, tuple)) else values
-        received.append(
-            lax.ppermute(value, axis, [(i, i ^ (base * m)) for i in range(count)])
-        )
+        pairs = [
+            (i * peers + h, (i ^ (m * (odd if h % 2 else even))) * peers + h)
+            for i in range(count)
+            for h in range(peers)
+        ]
+        received.append(lax.ppermute(value, ("ctx", "head"), pairs))
+    return received
+
+
+def exchange(values, peers):
+    received = []
+    for m in range(1, peers):
+        value = values[m - 1] if isinstance(values, (list, tuple)) else values
+        received.append(lax.ppermute(value, "head", [(i, i ^ m) for i in range(peers)]))
     return received
 
 
@@ -79,7 +112,7 @@
     return (4 << 20) + 3 * size
 
 
-def call(body, outs, args, flops=0, in_specs=None, out_specs=None, scratch=(), aliases=None):
+def call(body, outs, args, flops=0, in_specs=None, out_specs=None, scratch=()):
     size = sum(4 * a.size for a in args) + sum(4 * o.size for o in outs)
     kwargs = {}
     if in_specs is not None:
@@ -91,7 +124,6 @@
         body,
         out_shape=outs,
         scratch_shapes=scratch,
-        input_output_aliases=aliases or {},
         cost_estimate=pl.CostEstimate(flops=flops, bytes_accessed=size, transcendentals=0),
         compiler_params=pltpu.CompilerParams(vmem_limit_bytes=grant(size)),
         **kwargs,
@@ -187,25 +219,61 @@
         norm[at] = total[:, width:]
 
 
-def scan_body(base, radix, local, *refs):
-    received, (total, before) = refs[: radix - 1], refs[radix - 1 :]
-    mine = (lax.axis_index("ctx") // base) % radix
-    whole_sum, earlier = local[...], jnp.zeros(local.shape, F32)
+def counts(prefix, mine, m):
+    return (mine ^ m) < mine if prefix else (mine ^ m) > mine
+
+
+def step_body(now, after, ups, prefix, first, final, heads, local, *refs):
+    held, refs = ([], refs) if first else (refs[:2], refs[2:])
+    received, refs = refs[: now[2] - 1], refs[now[2] - 1 :]
+    weights, refs = refs[:heads], refs[heads:]
+    up, mine, then = is_up(ups), position(now), position(after)
+    own = local[...]
+    size = own.shape[0]
+    total = own if first else held[1][...]
+    part = jnp.zeros(own.shape, F32) if first else held[0][...]
     for m, piece in enumerate(received, 1):
         value = piece[...]
-        whole_sum = whole_sum + value
-        earlier = earlier + jnp.where((mine ^ m) < mine, value, 0.0)
-    total[...] = whole_sum
-    before[...] = earlier
-
-
-def scan_last_body(base, radix, before, *refs):
-    received, (result,) = refs[: radix - 1], refs[radix - 1 :]
-    mine = (lax.axis_index("ctx") // base) % radix
-    earlier = before[...]
+        total = total + value
+        take = counts(prefix, mine, m)
+        if not first:
+            take = jnp.logical_or(take, jnp.logical_not(up))
+        part = part + jnp.where(take, value, 0.0)
+    refs[0][...] = part
+    if not final:
+        refs[1][...] = total
+    refs = refs[1 if final else 2 :]
+    if heads:
+        scratch, kept, refs = refs[-1], refs[0], refs[1:-1]
+        width = weights[0].shape[0]
+        shard = kept.shape[0]
+        for h, weight in enumerate(weights):
+            scratch[h * width : (h + 1) * width] = weight[...]
+        rows = lambda m: pl.ds(pl.multiple_of((then ^ m) * shard, 8), shard)
+        kept[...] = scratch[rows(0), :]
+    for m, message in enumerate(refs, 1):
+        falling = part + jnp.where(counts(prefix, then, m), 0.0, own)
+        message[0:size] = jnp.where(up, total, falling)
+        if heads:
+            message[size:] = scratch[rows(m), :]
+
+
+def last_body(now, ups, prefix, part, *refs):
+    received, refs = refs[: now[2] - 1], refs[now[2] - 1 :]
+    up, mine = is_up(ups), position(now)
+    total = part[...]
+    size = total.shape[0]
     for m, piece in enumerate(received, 1):
-        earlier = earlier + jnp.where((mine ^ m) < mine, piece[...], 0.0)
-    result[...] = earlier
+        take = jnp.logical_or(counts(prefix, mine, m), jnp.logical_not(up))
+        total = total + jnp.where(take, piece[0:size], 0.0)
+    refs[-1][...] = total
+
+
+def shard_sum_body(size, kept, *refs):
+    total = kept[...]
+    for piece in refs[:-1]:
+        total = total + piece[size:]
+    refs[-1][...] = total
 
 
 def inter_body(heads, peers, share, *refs):
@@ -247,10 +315,10 @@
 
 
 def query_grad_body(
-    block, first, queries, weight, values, key_high, key_low, feat_high, feat_low,
+    block, first, queries, values, key_high, key_low, feat_high, feat_low,
     score_high, score_low, grads, state_high, state_low, *refs,
 ):
-    earlier, (grad_input, grad_weight, grad_key) = refs[1:-3], refs[-3:]
+    earlier, (logit_ref, grad_weight, grad_key) = refs[:-3], refs[-3:]
     rows, width = values.shape
     wide = key_high.shape[1]
     both = grads[...]
@@ -282,9 +350,9 @@
             key_sums[j] = key_term if key_sums[j] is None else key_sums[j] + key_term
             value_sums[j] = value_term if value_sums[j] is None else value_sums[j] + value_term
         logit_parts.append(logit_grad(joined(cut(feat, at)), grad_query))
-    grad_logits = split(jnp.concatenate(logit_parts, axis=0))
-    grad_input[...] = dot3(grad_logits, split(weight[0]), NT)
-    grad_weight[...] = dot3(split(queries[...]), grad_logits, TN)
+    grad_logits = jnp.concatenate(logit_parts, axis=0)
+    logit_ref[...] = grad_logits
+    grad_weight[...] = dot3(split(queries[...]), split(grad_logits), TN)
     for j in range(count):
         past = slice(j * block, (j + 1) * block)
         if first:
@@ -295,44 +363,20 @@
             grad_key[past, wide:] = earlier[0][past, wide:] + value_sums[j]
 
 
+def query_out_body(heads, weights, *refs):
+    logits, result = refs[:heads], refs[heads]
+    width = weights.shape[1]
+    for h in range(heads):
+        result[:, h * width : (h + 1) * width] = dot3(
+            split(logits[h][...]), split(weights[h]), NT
+        )
+
+
 def sum_body(*refs):
     total = refs[0][...]
     for piece in refs[1:-1]:
         total = total + piece[...]
     refs[-1][...] = total
-
-
-def suffix_weight_body(base, radix, above, heads, local, *refs):
-    received, refs = refs[: above - 1], refs[above - 1 :]
-    weights, (later, kept, *messages) = refs[:heads], refs[heads:]
-    scratch = messages.pop()
-    mine = (lax.axis_index("ctx") // base) % radix
-    upper = (lax.axis_index("ctx") // (base * radix)) % above
-    size = local.shape[0]
-    width = weights[0].shape[0]
-    shard = heads * width // radix
-    for h, weight in enumerate(weights):
-        scratch[h * width : (h + 1) * width] = weight[...]
-    total = jnp.zeros(local.shape, F32)
-    for m, piece in enumerate(received, 1):
-        total = total + jnp.where((upper ^ m) > upper, piece[...], 0.0)
-    later[...] = total
-    rows = lambda m: pl.ds(pl.multiple_of((mine ^ m) * shard, 8), shard)
-    kept[...] = scratch[rows(0), :]
-    for m, message in enumerate(messages, 1):
-        message[0:size] = total + jnp.where(mine > (mine ^ m), local[...], 0.0)
-        message[size : size + shard] = scratch[rows(m), :]
-
-
-def suffix_last_body(later, kept, *refs):
-    received, (result, shard) = refs[:-2], refs[-2:]
-    size = later.shape[0]
-    total, sums = later[...], kept[...]
-    for piece in received:
-        total = total + piece[0:size]
-        sums = sums + piece[size : size + sums.shape[0]]
-    result[...] = total
-    shard[...] = sums
 
 
 def key_grad_body(share, piece, inner, values, keys, key_high, key_low, *refs):
@@ -387,17 +431,21 @@
     message[rows:] = shard[...]
 
 
-def weight_last_body(base, radix, rows, local, *refs):
-    received, (share, gathered) = refs[: radix - 1], refs[radix - 1 :]
-    mine = (lax.axis_index("ctx") // base) % radix
-    total = local[0:rows]
-    shard = local.shape[0] - rows
-    gathered[pl.ds(pl.multiple_of(mine * shard, 8), shard), :] = local[rows:]
-    for m, piece in enumerate(received, 1):
+def weight_share_body(rows, *refs):
+    pieces, share = refs[:-1], refs[-1]
+    total = pieces[0][0:rows]
+    for piece in pieces[1:]:
         total = total + piece[0:rows]
+    share[...] = total
+
+
+def weight_gather_body(now, rows, *refs):
+    pieces, gathered = refs[:-1], refs[-1]
+    mine = position(now)
+    shard = pieces[0].shape[0] - rows
+    for m, piece in enumerate(pieces):
         at = pl.ds(pl.multiple_of((mine ^ m) * shard, 8), shard)
         gathered[at, :] = piece[rows:]
-    share[...] = total
 
 
 def gather_body(rows, *refs):
@@ -415,7 +463,8 @@
     share = width // peers
     part = rows // peers
     block = min(256, rows)
-    digits = digits_of(lax.axis_size("ctx"))
+    rising, rising_ups = rounds_of(lax.axis_size("ctx"), peers, True)
+    falling, falling_ups = rounds_of(lax.axis_size("ctx"), peers, False)
     message = (2 * share + 8, half)
     bind = functools.partial
     unit = 2 * rows * width * wide
@@ -430,7 +479,7 @@
     key_high, key_low, local = call(
         bind(key_body, share),
         [feat_shape, feat_shape, out(message)],
-        (keys, values, k_feature),
+        [pltpu.with_memory_space_constraint(x, pltpu.HBM) for x in (keys, values, k_feature)],
         6 * unit,
         [hbm] * 3,
         scratch=[
@@ -442,24 +491,48 @@
         ],
     )
 
-    before, total = None, local
-    for place, (base, radix) in enumerate(digits):
-        received = exchange(total, "ctx", base, radix)
-        if place == 0:
-            total, before = call(
-                bind(scan_body, base, radix), [out(message)] * 2, (total, *received)
+    def neighbor_sum(local, rounds, ups, prefix, weights=()):
+        heads_now, kept = 0, None
+        held, values = (), local
+        for place, now in enumerate(rounds[:-1]):
+            received = swap(values, now)
+            after = rounds[place + 1]
+            tall = message
+            final = place + 2 == len(rounds)
+            outs, scratch = [out(message)] * (1 if final else 2), []
+            extra = ()
+            if final and weights:
+                heads_now = len(weights)
+                shard = heads_now * width // after[2]
+                outs.append(out((shard, half)))
+                tall = (message[0] + shard, half)
+                scratch = [pltpu.VMEM((heads_now * width, half), F32)]
+                extra = tuple(weights)
+            results = call(
+                bind(step_body, now, after, ups, prefix, place == 0, final, heads_now),
+                outs + [out(tall)] * (after[2] - 1),
+                (local, *held, *received, *extra),
+                scratch=scratch,
             )
-        else:
-            (before,) = call(bind(scan_last_body, base, radix), [out(message)], (before, *received))
-            if place + 1 < len(digits):
-                total = sum(received, total)
-    prefix = [before] + exchange(before, "head", 1, peers)
-
-    def head_specs(h):
-        return [
-            pl.BlockSpec((rows, width), lambda i: (0, h)),
-            pl.BlockSpec((1, width, half), lambda i: (h, 0, 0)),
-        ]
+            keep = 1 if final else 2
+            held, results = tuple(results[:keep]), results[keep:]
+            if extra:
+                kept, results = results[0], results[1:]
+            values = results
+        received = swap(values, rounds[-1])
+        (result,) = call(
+            bind(last_body, rounds[-1], ups, prefix), [out(message)], (held[0], *received)
+        )
+        if kept is None:
+            return result, None
+        (shard_sum,) = call(bind(shard_sum_body, message[0]), [out(kept.shape)], (kept, *received))
+        return result, shard_sum
+
+    before, _ = neighbor_sum(local, rising, rising_ups, True)
+    prefix = [before] + exchange(before, peers)
+
+    def query_spec(h):
+        return pl.BlockSpec((rows, width), lambda i: (0, h))
 
     feats, scores, inner = [], [], []
     for h in range(heads):
@@ -472,7 +545,8 @@
             outs,
             args,
             9 * unit,
-            head_specs(h) + [whole(a.shape) for a in args[2:]],
+            [query_spec(h), pl.BlockSpec((1, width, half), lambda i, h=h: (h, 0, 0))]
+            + [whole(a.shape) for a in args[2:]],
             [whole(o.shape) for o in outs],
         )
         feats.append(results[0:2])
@@ -495,73 +569,34 @@
     )
     state, results = results[:2], results[2:]
     grads, results = results[:heads], results[heads:]
-    sends = exchange(results[1:], "head", 1, peers)
+    sends = exchange(results[1:], peers)
     (carried,) = call(sum_body, [out(message)], (results[0], *sends))
 
-    weight_grads = []
-    grad_queries = key_inner = None
+    weight_grads, query_logits, key_inner = [], [], None
     for h in range(heads):
-        args = [
-            queries, q_feature, values, key_high, key_low, *feats[h], *scores[h], grads[h], *state,
-        ]
-        outs = [
-            out((rows, heads * width)), out((width, half)), out((rows, wide + width)),
-        ]
-        specs = head_specs(h) + [whole(a.shape) for a in args[2:]]
-        aliases = {}
+        args = [queries, values, key_high, key_low, *feats[h], *scores[h], grads[h], *state]
+        outs = [out((rows, half)), out((width, half)), out((rows, wide + width))]
         if h > 0:
-            aliases = {len(args): 0}
-            args += [grad_queries, key_inner]
-            specs += [pl.BlockSpec(memory_space=pl.ANY), whole(key_inner.shape)]
-        grad_queries, grad_weight, key_inner = call(
+            args.append(key_inner)
+        logits, grad_weight, key_inner = call(
             bind(query_grad_body, block, h == 0),
             outs,
             args,
-            15 * unit,
-            specs,
-            [head_specs(h)[0]] + [whole(o.shape) for o in outs[1:]],
-            aliases=aliases,
+            14 * unit,
+            [query_spec(h)] + [whole(a.shape) for a in args[1:]],
+            [whole(o.shape) for o in outs],
         )
+        query_logits.append(logits)
         weight_grads.append(grad_weight)
-
-    later, messages = None, carried
-    base_low, radix_low = digits[0]
-    shard = heads * width // radix_low
-    for place in range(len(digits) - 1, 0, -1):
-        base, radix = digits[place]
-        received = exchange(messages, "ctx", base, radix)
-        below_base, below_radix = digits[place - 1]
-        if place == 1 and len(digits) == 2:
-            results = call(
-                bind(suffix_weight_body, base_low, radix_low, radix, heads),
-                [out(message), out((shard, half))]
-                + [out((message[0] + shard, half))] * (radix_low - 1),
-                (carried, *received, *weight_grads),
-                scratch=[pltpu.VMEM((heads * width, half), F32)],
-            )
-            later, kept, messages = results[0], results[1], results[2:]
-        else:
-            mine = (lax.axis_index("ctx") // base) % radix
-            if place == len(digits) - 1:
-                later = sum(jnp.where((mine ^ m) > mine, r, 0.0) for m, r in enumerate(received, 1))
-            else:
-                later = sum(received, later)
-            below = (lax.axis_index("ctx") // below_base) % below_radix
-            messages = [
-                later + jnp.where(below > (below ^ m), carried, 0.0) for m in range(1, below_radix)
-            ]
-            if place == 1:
-                stacked = jnp.concatenate(weight_grads, axis=0)
-                cut = lambda m: lax.dynamic_slice_in_dim(stacked, (below ^ m) * shard, shard, 0)
-                kept = cut(0)
-                messages = [
-                    jnp.concatenate([part_message, cut(m)], axis=0)
-                    for m, part_message in enumerate(messages, 1)
-                ]
-    received = exchange(messages, "ctx", base_low, radix_low)
-    later, q_shard = call(
-        suffix_last_body, [out(message), out((shard, half))], (later, kept, *received)
-    )
+    (grad_queries,) = call(
+        bind(query_out_body, heads),
+        [out((rows, heads * width))],
+        (q_feature, *query_logits),
+        3 * unit,
+    )
+
+    later, q_shard = neighbor_sum(carried, falling, falling_ups, False, weight_grads)
+    shard = q_shard.shape[0]
 
     weight_rows = width // peers
     results = call(
@@ -575,7 +610,7 @@
     )
     key_logits, later_high, later_low = results[:3]
     weight_parts = results[3:]
-    weight_parts = [weight_parts[0]] + exchange(weight_parts[1:], "head", 1, peers)
+    weight_parts = [weight_parts[0]] + exchange(weight_parts[1:], peers)
     (total,) = call(
         weight_message_body, [out((weight_rows + shard, half))], (*weight_parts, q_shard)
     )
@@ -586,20 +621,22 @@
         6 * unit,
         scratch=[pltpu.VMEM((rows, 2 * width), F32)],
     )
-    key_parts = [key_parts[0]] + exchange(key_parts[1:], "head", 1, peers)
+    key_parts = [key_parts[0]] + exchange(key_parts[1:], peers)
     grad_keys, grad_values = call(key_sum_body, [out((part, width))] * 2, key_parts)
-    for place in range(len(digits) - 1, 0, -1):
-        base, radix = digits[place]
-        received = exchange(total, "ctx", base, radix)
+    for now in falling[:-1]:
+        received = swap(total, now)
         (total,) = call(sum_body, [out(total.shape)], (total, *received))
-    received = exchange(total, "ctx", base_low, radix_low)
-    k_share, q_sum = call(
-        bind(weight_last_body, base_low, radix_low, weight_rows),
-        [out((weight_rows, half)), out((heads * width, half))],
+    received = swap(total, falling[-1])
+    (k_share,) = call(
+        bind(weight_share_body, weight_rows), [out((weight_rows, half))], (total, *received)
+    )
+    shares = [k_share] + exchange(k_share, peers)
+    (k_sum,) = call(bind(gather_body, weight_rows), [out((width, half))], shares)
+    (q_sum,) = call(
+        bind(weight_gather_body, falling[-1], weight_rows),
+        [out((heads * width, half))],
         (total, *received),
     )
-    shares = [k_share] + exchange(k_share, "head", 1, peers)
-    (k_sum,) = call(bind(gather_body, weight_rows), [out((width, half))], shares)
     return (
         grad_queries,
         grad_keys,

time: 70.6 us -> 67.6 us (0.958)
  local copies, waits for them, and re-layouts: 3.65 us -> 0.92 us
  waiting for transfers between devices: 24.4 us -> 23.5 us
    unnamed x22 -> x16, local copies, waits for them, and re-layouts: 3.65 us -> 0.92 us
    ppermute x23, waiting for transfers between devices: 24.4 us -> 23.5 us  [the longest x18 21.2 us: swap(): received.append(lax.ppermute(value, ('ctx', 'head'), pairs))]
    pallas_call x18 -> x21, Pallas kernels: 15.5 us -> 16 us  [call(): pl.pallas_call(body, out_shape=outs, scratch_shapes=scratch, cost_estimat...]
  transfers between devices with their start and end apart: 23 -> 23, of which waited for: 16 -> 15; matrix products, arithmetic and copies ran while one was open for 0% -> 0% of each run, Pallas kernels for 14% -> 14%
where the time goes in v1:
time: 67.6 us; the launch traced here: 67.4 us
  starting transfers between devices  25.9 us (38%)
  waiting for transfers between devices  23.5 us (35%)
  Pallas kernels  16 us (24%)
  local copies, waits for them, and re-layouts  0.92 us (1%)
  between operations  0.89 us (1%)
    ppermute x18, starting transfers between devices, swap(): received.append(lax.ppermute(value, ('ctx', 'head'), pairs))  25.1 us
    ppermute x18, waiting for transfers between devices, swap(): received.append(lax.ppermute(value, ('ctx', 'head'), pairs))  21.2 us
    pallas_call x21, Pallas kernels, call(): pl.pallas_call(body, out_shape=outs, scratch_shapes=scratch, cost_estimat...  16 us
    ppermute x5, waiting for transfers between devices, exchange(): lax.ppermute(value, 'head', [(i, i ^ m) for i in range(peers)])  2.31 us
  transfers between devices with their start and end apart: 23, of which 15 were waited for; matrix products, arithmetic and copies ran while one was open for 0% of the time, Pallas kernels for 14%

profile of v1, /device:TPU:0, one launch (start us, length us, event | category | flops | bytes accessed | tf_op | source)
XLA Modules:
  0.0 67.4 jit_solution(12894745407482277202)
XLA Ops:
  0.6 2.4 %shard_map.119 = (bf16[512,256]{1,0:T(8,128)(2,1)S(1)}, bf16[512,256]{1,0:T(8,128)(2,1)S(1)}, f32[136,128]{1,0:T(8,128)S(1)}) custom-call(f32[512,128]{1,0:T(8,128)} %keys.1, f32[512,128]{1,0:T(8,128)} %values.9, f32[128,128]{1,0:T(8,128)} %weight.5), custom_call_target="tpu_custom_call" | custom-call | flops 201326592 | bytes 1708032 | tf_op jit(solution)/shard_map/pallas_call | solution.py:123
  3.1 4.0 %collective-permute-start.2 = (f32[136,128]{1,0:T(8,128)S(1)}, f32[136,128]{1,0:T(8,128)S(1)}, u32[]{:S(2)}, u32[]{:S(2)}) collective-permute-start(f32[136,128]{1,0:T(8,128)S(1)} %get-tuple-element.56.local), channel_id=1, source_target_pairs={{0,6},{1,25},{2,4},{3,27},{4,2},{5,29},{6,0},{7,31},{8,14},{9,17},... | collective-permute-start | bytes 208904 | tf_op jit(solution)/shard_map/ppermute | solution.py:99
  7.7 1.6 %collective-permute-done.2.refs_2_ = f32[136,128]{1,0:T(8,128)S(1)} collective-permute-done((f32[136,128]{1,0:T(8,128)S(1)}, f32[136,128]{1,0:T(8,128)S(1)}, u32[]{:S(2)}, u32[]{:S(2)}) %collective-permute-start.2) | collective-permute-done | bytes 69664 | tf_op jit(solution)/shard_map/ppermute | solution.py:99
  9.3 2.0 %collective-permute-done.1.refs_1_ = f32[136,128]{1,0:T(8,128)S(1)} collective-permute-done((f32[136,128]{1,0:T(8,128)S(1)}, f32[136,128]{1,0:T(8,128)S(1)}, u32[]{:S(2)}, u32[]{:S(2)}) %collective-permute-start.1) | collective-permute-done | bytes 69664 | tf_op jit(solution)/shard_map/ppermute | solution.py:99
  11.9 1.6 %collective-permute-start.3 = (f32[136,128]{1,0:T(8,128)S(1)}, f32[136,128]{1,0:T(8,128)S(1)}, u32[]{:S(2)}, u32[]{:S(2)}) collective-permute-start(f32[136,128]{1,0:T(8,128)S(1)} %get-tuple-element.58), channel_id=1, source_target_pairs={{0,8},{1,3},{2,10},{3,1},{4,12},{5,7},{6,14},{7,5},{8,0},{9,11},{1... | collective-permute-start | bytes 208904 | tf_op jit(solution)/shard_map/ppermute | solution.py:99
  13.6 2.6 %collective-permute-start.4 = (f32[136,128]{1,0:T(8,128)S(1)}, f32[136,128]{1,0:T(8,128)S(1)}, u32[]{:S(2)}, u32[]{:S(2)}) collective-permute-start(f32[136,128]{1,0:T(8,128)S(1)} %get-tuple-element.59), channel_id=1, source_target_pairs={{0,16},{1,5},{2,18},{3,7},{4,20},{5,1},{6,22},{7,3},{8,24},{9,13},... | collective-permute-start | bytes 208904 | tf_op jit(solution)/shard_map/ppermute | solution.py:99
  16.5 3.0 %collective-permute-done.4.refs_1_ = f32[136,128]{1,0:T(8,128)S(1)} collective-permute-done((f32[136,128]{1,0:T(8,128)S(1)}, f32[136,128]{1,0:T(8,128)S(1)}, u32[]{:S(2)}, u32[]{:S(2)}) %collective-permute-start.4) | collective-permute-done | bytes 69664 | tf_op jit(solution)/shard_map/ppermute | solution.py:99
  19.5 2.7 %collective-permute-done.5.refs_2_ = f32[136,128]{1,0:T(8,128)S(1)} collective-permute-done((f32[136,128]{1,0:T(8,128)S(1)}, f32[136,128]{1,0:T(8,128)S(1)}, u32[]{:S(2)}, u32[]{:S(2)}) %collective-permute-start.5) | collective-permute-done | bytes 69664 | tf_op jit(solution)/shard_map/ppermute | solution.py:99
  23.4 1.6 %shard_map.123 = (bf16[512,256]{1,0:T(8,128)(2,1)S(1)}, bf16[512,256]{1,0:T(8,128)(2,1)S(1)}, bf16[512,512]{1,0:T(8,128)(2,1)S(1)}, bf16[512,512]{1,0:T(8,128)(2...) custom-call(f32[512,256]{1,0:T(8,128)S(1)} %copy-done, f32[2,128,128]{2,1,0:T(8,128)S(1)} %copy-done.2, ...), custom_call_target="tpu_custom_call" | custom-call | flops 301989888 | bytes 5636096 | tf_op jit(solution)/shard_map/pallas_call | solution.py:123
  25.1 1.6 %shard_map.120 = (bf16[512,256]{1,0:T(8,128)(2,1)S(1)}, bf16[512,256]{1,0:T(8,128)(2,1)S(1)}, bf16[512,512]{1,0:T(8,128)(2,1)S(1)}, bf16[512,512]{1,0:T(8,128)(2...) custom-call(f32[512,256]{1,0:T(8,128)S(1)} %copy-done, f32[2,128,128]{2,1,0:T(8,128)S(1)} %copy-done.2, ...), custom_call_target="tpu_custom_call" | custom-call | flops 301989888 | bytes 5636096 | tf_op jit(solution)/shard_map/pallas_call | solution.py:123
  26.7 1.6 %shard_map.124 = (bf16[256,256]{1,0:T(8,128)(2,1)S(1)}, bf16[256,256]{1,0:T(8,128)(2,1)S(1)}, f32[512,256]{1,0:T(8,128)S(1)}, f32[512,256]{1,0:T(8,128)S(1)}, f3...) custom-call(f32[136,128]{1,0:T(8,128)S(1)} %shard_map.122.refs_0_, f32[136,128]{1,0:T(8,128)S(1)} %collective-permute-done.6.refs_1_, ...), custom_call_target="tpu_custom_call" | custom-call | flops 805306368 | bytes 5521408 | tf_op jit(solution)/shard_map/pallas_call | solution.py:123
  28.4 1.2 %collective-permute-done.7.refs_1_ = f32[136,128]{1,0:T(8,128)S(1)} collective-permute-done((f32[136,128]{1,0:T(8,128)S(1)}, f32[136,128]{1,0:T(8,128)S(1)}, u32[]{:S(2)}, u32[]{:S(2)}) %collective-permute-start.7) | collective-permute-done | bytes 69664 | tf_op jit(solution)/shard_map/ppermute | solution.py:107
  30.6 3.5 %collective-permute-start.8 = (f32[136,128]{1,0:T(8,128)S(1)}, f32[136,128]{1,0:T(8,128)S(1)}, u32[]{:S(2)}, u32[]{:S(2)}) collective-permute-start(f32[136,128]{1,0:T(8,128)S(1)} %shard_map.128.local), channel_id=1, source_target_pairs={{0,8},{1,3},{2,10},{3,1},{4,12},{5,7},{6,14},{7,5},{8,0},{9,11},{1... | collective-permute-start | bytes 208904 | tf_op jit(solution)/shard_map/ppermute | solution.py:99
  34.1 2.0 %shard_map.125 = (f32[512,128]{1,0:T(8,128)S(1)}, f32[128,128]{1,0:T(8,128)S(1)}, f32[512,384]{1,0:T(8,128)S(1)}) custom-call(f32[512,256]{1,0:T(8,128)S(1)} %copy-done, f32[512,128]{1,0:T(8,128)S(1)} %copy-done.1, bf16[512,256]{1,0:T(8,128)(2,1)S(1)} %get-tuple-element.50.key_high, bf16[512,256]{1,0:T(8,128)(2,1)S(1)} %get-tuple-element.51.key_low, ...), custom_call_target="tpu_custom_call" | custom-call | flops 469762048 | bytes 7143424 | tf_op jit(solution)/shard_map/pallas_call | solution.py:123
  36.1 2.0 %shard_map.126 = (f32[512,128]{1,0:T(8,128)S(1)}, f32[128,128]{1,0:T(8,128)S(1)}, f32[512,384]{1,0:T(8,128)S(1)}) custom-call(f32[512,256]{1,0:T(8,128)S(1)} %copy-done, f32[512,128]{1,0:T(8,128)S(1)} %copy-done.1, bf16[512,256]{1,0:T(8,128)(2,1)S(1)} %get-tuple-element.50.key_high, bf16[512,256]{1,0:T(8,128)(2,1)S(1)} %get-tuple-element.51.key_low, ...), custom_call_target="tpu_custom_call" | custom-call | flops 469762048 | bytes 7929856 | tf_op jit(solution)/shard_map/pallas_call | solution.py:123
  38.8 1.5 %collective-permute-start.12 = (f32[200,128]{1,0:T(8,128)S(1)}, f32[200,128]{1,0:T(8,128)S(1)}, u32[]{:S(2)}, u32[]{:S(2)}) collective-permute-start(f32[200,128]{1,0:T(8,128)S(1)} %get-tuple-element.82), channel_id=1, source_target_pairs={{0,4},{1,17},{2,6},{3,19},{4,0},{5,21},{6,2},{7,23},{8,12},{9,25},... | collective-permute-start | bytes 307208 | tf_op jit(solution)/shard_map/ppermute | solution.py:99
  40.3 1.4 %collective-permute-start.13 = (f32[200,128]{1,0:T(8,128)S(1)}, f32[200,128]{1,0:T(8,128)S(1)}, u32[]{:S(2)}, u32[]{:S(2)}) collective-permute-start(f32[200,128]{1,0:T(8,128)S(1)} %get-tuple-element.83), channel_id=1, source_target_pairs={{0,6},{1,25},{2,4},{3,27},{4,2},{5,29},{6,0},{7,31},{8,14},{9,17},... | collective-permute-start | bytes 307208 | tf_op jit(solution)/shard_map/ppermute | solution.py:99
  43.5 2.4 %collective-permute-done.13.refs_2_ = f32[200,128]{1,0:T(8,128)S(1)} collective-permute-done((f32[200,128]{1,0:T(8,128)S(1)}, f32[200,128]{1,0:T(8,128)S(1)}, u32[]{:S(2)}, u32[]{:S(2)}) %collective-permute-start.13) | collective-permute-done | bytes 102432 | tf_op jit(solution)/shard_map/ppermute | solution.py:99
  50.8 2.6 %collective-permute-start.16 = (f32[128,128]{1,0:T(8,128)S(1)}, f32[128,128]{1,0:T(8,128)S(1)}, u32[]{:S(2)}, u32[]{:S(2)}) collective-permute-start(f32[128,128]{1,0:T(8,128)S(1)} %shard_map.135.refs_0_), channel_id=1, source_target_pairs={{0,8},{1,3},{2,10},{3,1},{4,12},{5,7},{6,14},{7,5},{8,0},{9,11},{1... | collective-permute-start | bytes 196616 | tf_op jit(solution)/shard_map/ppermute | solution.py:99
  53.5 1.8 %collective-permute-done.18.refs_3_ = f32[128,128]{1,0:T(8,128)S(1)} collective-permute-done((f32[128,128]{1,0:T(8,128)S(1)}, f32[128,128]{1,0:T(8,128)S(1)}, u32[]{:S(2)}, u32[]{:S(2)}) %collective-permute-start.18) | collective-permute-done | bytes 65568 | tf_op jit(solution)/shard_map/ppermute | solution.py:99
  56.5 1.6 %collective-permute-start.21 = (f32[128,128]{1,0:T(8,128)S(1)}, f32[128,128]{1,0:T(8,128)S(1)}, u32[]{:S(2)}, u32[]{:S(2)}) collective-permute-start(f32[128,128]{1,0:T(8,128)S(1)} %shard_map.136.refs_0_), channel_id=1, source_target_pairs={{0,6},{1,25},{2,4},{3,27},{4,2},{5,29},{6,0},{7,31},{8,14},{9,17},... | collective-permute-start | bytes 196616 | tf_op jit(solution)/shard_map/ppermute | solution.py:99
  58.1 1.7 %collective-permute-start.20 = (f32[128,128]{1,0:T(8,128)S(1)}, f32[128,128]{1,0:T(8,128)S(1)}, u32[]{:S(2)}, u32[]{:S(2)}) collective-permute-start(f32[128,128]{1,0:T(8,128)S(1)} %shard_map.136.refs_0_), channel_id=1, source_target_pairs={{0,4},{1,17},{2,6},{3,19},{4,0},{5,21},{6,2},{7,23},{8,12},{9,25},... | collective-permute-start | bytes 196616 | tf_op jit(solution)/shard_map/ppermute | solution.py:99
  60.1 1.7 %collective-permute-done.21.refs_3_ = f32[128,128]{1,0:T(8,128)S(1)} collective-permute-done((f32[128,128]{1,0:T(8,128)S(1)}, f32[128,128]{1,0:T(8,128)S(1)}, u32[]{:S(2)}, u32[]{:S(2)}) %collective-permute-start.21) | collective-permute-done | bytes 65568 | tf_op jit(solution)/shard_map/ppermute | solution.py:99
  62.4 1.7 %collective-permute-done.19.refs_1_ = f32[128,128]{1,0:T(8,128)S(1)} collective-permute-done((f32[128,128]{1,0:T(8,128)S(1)}, f32[128,128]{1,0:T(8,128)S(1)}, u32[]{:S(2)}, u32[]{:S(2)}) %collective-permute-start.19) | collective-permute-done | bytes 65568 | tf_op jit(solution)/shard_map/ppermute | solution.py:99
  (61 shorter events, 16.4 us)
Async XLA Ops:
  0.6 21.8 %copy-start.5 = (f32[512,256]{1,0:T(8,128)S(1)}, f32[512,256]{1,0:T(8,128)}, u32[]{:S(2)}) copy-start(f32[512,256]{1,0:T(8,128)} %param.11) | copy-start | bytes 1572868
  3.1 6.3 %collective-permute-start.2 = (f32[136,128]{1,0:T(8,128)S(1)}, f32[136,128]{1,0:T(8,128)S(1)}, u32[]{:S(2)}, u32[]{:S(2)}) collective-permute-start(f32[136,128]{1,0:T(8,128)S(1)} %get-tuple-element.56.local), channel_id=1, source_target_pairs={{0,6},{1,25},{2,4},{3,27},{4,2},{5,29},{6,0},{7,31},{8,14},{9,17},... | collective-permute-start | bytes 208904 | tf_op jit(solution)/shard_map/ppermute | solution.py:99
  7.0 4.3 %collective-permute-start.1 = (f32[136,128]{1,0:T(8,128)S(1)}, f32[136,128]{1,0:T(8,128)S(1)}, u32[]{:S(2)}, u32[]{:S(2)}) collective-permute-start(f32[136,128]{1,0:T(8,128)S(1)} %get-tuple-element.56.local), channel_id=1, source_target_pairs={{0,4},{1,17},{2,6},{3,19},{4,0},{5,21},{6,2},{7,23},{8,12},{9,25},... | collective-permute-start | bytes 208904 | tf_op jit(solution)/shard_map/ppermute | solution.py:99
  7.5 4.3 %collective-permute-start = (f32[136,128]{1,0:T(8,128)S(1)}, f32[136,128]{1,0:T(8,128)S(1)}, u32[]{:S(2)}, u32[]{:S(2)}) collective-permute-start(f32[136,128]{1,0:T(8,128)S(1)} %get-tuple-element.56.local), channel_id=1, source_target_pairs={{0,2},{1,9},{2,0},{3,11},{4,6},{5,13},{6,4},{7,15},{8,10},{9,1},{1... | collective-permute-start | bytes 208904 | tf_op jit(solution)/shard_map/ppermute | solution.py:99
  11.9 4.6 %collective-permute-start.3 = (f32[136,128]{1,0:T(8,128)S(1)}, f32[136,128]{1,0:T(8,128)S(1)}, u32[]{:S(2)}, u32[]{:S(2)}) collective-permute-start(f32[136,128]{1,0:T(8,128)S(1)} %get-tuple-element.58), channel_id=1, source_target_pairs={{0,8},{1,3},{2,10},{3,1},{4,12},{5,7},{6,14},{7,5},{8,0},{9,11},{1... | collective-permute-start | bytes 208904 | tf_op jit(solution)/shard_map/ppermute | solution.py:99
  13.6 6.0 %collective-permute-start.4 = (f32[136,128]{1,0:T(8,128)S(1)}, f32[136,128]{1,0:T(8,128)S(1)}, u32[]{:S(2)}, u32[]{:S(2)}) collective-permute-start(f32[136,128]{1,0:T(8,128)S(1)} %get-tuple-element.59), channel_id=1, source_target_pairs={{0,16},{1,5},{2,18},{3,7},{4,20},{5,1},{6,22},{7,3},{8,24},{9,13},... | collective-permute-start | bytes 208904 | tf_op jit(solution)/shard_map/ppermute | solution.py:99
  16.2 6.1 %collective-permute-start.5 = (f32[136,128]{1,0:T(8,128)S(1)}, f32[136,128]{1,0:T(8,128)S(1)}, u32[]{:S(2)}, u32[]{:S(2)}) collective-permute-start(f32[136,128]{1,0:T(8,128)S(1)} %get-tuple-element.60), channel_id=1, source_target_pairs={{0,24},{1,7},{2,26},{3,5},{4,28},{5,3},{6,30},{7,1},{8,16},{9,15},... | collective-permute-start | bytes 208904 | tf_op jit(solution)/shard_map/ppermute | solution.py:99
  22.3 4.3 %collective-permute-start.6 = (f32[136,128]{1,0:T(8,128)S(1)}, f32[136,128]{1,0:T(8,128)S(1)}, u32[]{:S(2)}, u32[]{:S(2)}) collective-permute-start(f32[136,128]{1,0:T(8,128)S(1)} %shard_map.122.refs_0_), channel_id=1, source_target_pairs={{0,1},{1,0},{2,3},{3,2},{4,5},{5,4},{6,7},{7,6},{8,9},{9,8},{10,11... | collective-permute-start | bytes 208904 | tf_op jit(solution)/shard_map/ppermute | solution.py:107
  28.3 1.3 %collective-permute-start.7 = (f32[136,128]{1,0:T(8,128)S(1)}, f32[136,128]{1,0:T(8,128)S(1)}, u32[]{:S(2)}, u32[]{:S(2)}) collective-permute-start(f32[136,128]{1,0:T(8,128)S(1)} %get-tuple-element.77), channel_id=1, source_target_pairs={{0,1},{1,0},{2,3},{3,2},{4,5},{5,4},{6,7},{7,6},{8,9},{9,8},{10,11... | collective-permute-start | bytes 208904 | tf_op jit(solution)/shard_map/ppermute | solution.py:107
  29.7 8.4 %collective-permute-start.10 = (f32[136,128]{1,0:T(8,128)S(1)}, f32[136,128]{1,0:T(8,128)S(1)}, u32[]{:S(2)}, u32[]{:S(2)}) collective-permute-start(f32[136,128]{1,0:T(8,128)S(1)} %shard_map.128.local), channel_id=1, source_target_pairs={{0,24},{1,7},{2,26},{3,5},{4,28},{5,3},{6,30},{7,1},{8,16},{9,15},... | collective-permute-start | bytes 208904 | tf_op jit(solution)/shard_map/ppermute | solution.py:99
  30.6 7.5 %collective-permute-start.9 = (f32[136,128]{1,0:T(8,128)S(1)}, f32[136,128]{1,0:T(8,128)S(1)}, u32[]{:S(2)}, u32[]{:S(2)}) collective-permute-start(f32[136,128]{1,0:T(8,128)S(1)} %shard_map.128.local), channel_id=1, source_target_pairs={{0,16},{1,5},{2,18},{3,7},{4,20},{5,1},{6,22},{7,3},{8,24},{9,13},... | collective-permute-start | bytes 208904 | tf_op jit(solution)/shard_map/ppermute | solution.py:99
  30.6 7.5 %collective-permute-start.8 = (f32[136,128]{1,0:T(8,128)S(1)}, f32[136,128]{1,0:T(8,128)S(1)}, u32[]{:S(2)}, u32[]{:S(2)}) collective-permute-start(f32[136,128]{1,0:T(8,128)S(1)} %shard_map.128.local), channel_id=1, source_target_pairs={{0,8},{1,3},{2,10},{3,1},{4,12},{5,7},{6,14},{7,5},{8,0},{9,11},{1... | collective-permute-start | bytes 208904 | tf_op jit(solution)/shard_map/ppermute | solution.py:99
  38.2 4.7 %collective-permute-start.11 = (f32[200,128]{1,0:T(8,128)S(1)}, f32[200,128]{1,0:T(8,128)S(1)}, u32[]{:S(2)}, u32[]{:S(2)}) collective-permute-start(f32[200,128]{1,0:T(8,128)S(1)} %get-tuple-element.81), channel_id=1, source_target_pairs={{0,2},{1,9},{2,0},{3,11},{4,6},{5,13},{6,4},{7,15},{8,10},{9,1},{1... | collective-permute-start | bytes 307208 | tf_op jit(solution)/shard_map/ppermute | solution.py:99
  38.8 4.7 %collective-permute-start.12 = (f32[200,128]{1,0:T(8,128)S(1)}, f32[200,128]{1,0:T(8,128)S(1)}, u32[]{:S(2)}, u32[]{:S(2)}) collective-permute-start(f32[200,128]{1,0:T(8,128)S(1)} %get-tuple-element.82), channel_id=1, source_target_pairs={{0,4},{1,17},{2,6},{3,19},{4,0},{5,21},{6,2},{7,23},{8,12},{9,25},... | collective-permute-start | bytes 307208 | tf_op jit(solution)/shard_map/ppermute | solution.py:99
  40.3 5.6 %collective-permute-start.13 = (f32[200,128]{1,0:T(8,128)S(1)}, f32[200,128]{1,0:T(8,128)S(1)}, u32[]{:S(2)}, u32[]{:S(2)}) collective-permute-start(f32[200,128]{1,0:T(8,128)S(1)} %get-tuple-element.83), channel_id=1, source_target_pairs={{0,6},{1,25},{2,4},{3,27},{4,2},{5,29},{6,0},{7,31},{8,14},{9,17},... | collective-permute-start | bytes 307208 | tf_op jit(solution)/shard_map/ppermute | solution.py:99
  47.3 19.3 %collective-permute-start.14 = (f32[256,256]{1,0:T(8,128)S(1)}, f32[256,256]{1,0:T(8,128)S(1)}, u32[]{:S(2)}, u32[]{:S(2)}) collective-permute-start(f32[256,256]{1,0:T(8,128)S(1)} %get-tuple-element.89), channel_id=1, source_target_pairs={{0,1},{1,0},{2,3},{3,2},{4,5},{5,4},{6,7},{7,6},{8,9},{9,8},{10,11... | collective-permute-start | bytes 786440 | tf_op jit(solution)/shard_map/ppermute | solution.py:107
  47.4 1.6 %collective-permute-start.15 = (f32[64,128]{1,0:T(8,128)S(1)}, f32[64,128]{1,0:T(8,128)S(1)}, u32[]{:S(2)}, u32[]{:S(2)}) collective-permute-start(f32[64,128]{1,0:T(8,128)S(1)} %get-tuple-element.93), channel_id=1, source_target_pairs={{0,1},{1,0},{2,3},{3,2},{4,5},{5,4},{6,7},{7,6},{8,9},{9,8},{10,11... | collective-permute-start | bytes 98312 | tf_op jit(solution)/shard_map/ppermute | solution.py:107
  49.0 6.3 %collective-permute-start.18 = (f32[128,128]{1,0:T(8,128)S(1)}, f32[128,128]{1,0:T(8,128)S(1)}, u32[]{:S(2)}, u32[]{:S(2)}) collective-permute-start(f32[128,128]{1,0:T(8,128)S(1)} %shard_map.135.refs_0_), channel_id=1, source_target_pairs={{0,24},{1,7},{2,26},{3,5},{4,28},{5,3},{6,30},{7,1},{8,16},{9,15},... | collective-permute-start | bytes 196616 | tf_op jit(solution)/shard_map/ppermute | solution.py:99
  49.9 6.6 %collective-permute-start.17 = (f32[128,128]{1,0:T(8,128)S(1)}, f32[128,128]{1,0:T(8,128)S(1)}, u32[]{:S(2)}, u32[]{:S(2)}) collective-permute-start(f32[128,128]{1,0:T(8,128)S(1)} %shard_map.135.refs_0_), channel_id=1, source_target_pairs={{0,16},{1,5},{2,18},{3,7},{4,20},{5,1},{6,22},{7,3},{8,24},{9,13},... | collective-permute-start | bytes 196616 | tf_op jit(solution)/shard_map/ppermute | solution.py:99
  50.8 5.7 %collective-permute-start.16 = (f32[128,128]{1,0:T(8,128)S(1)}, f32[128,128]{1,0:T(8,128)S(1)}, u32[]{:S(2)}, u32[]{:S(2)}) collective-permute-start(f32[128,128]{1,0:T(8,128)S(1)} %shard_map.135.refs_0_), channel_id=1, source_target_pairs={{0,8},{1,3},{2,10},{3,1},{4,12},{5,7},{6,14},{7,5},{8,0},{9,11},{1... | collective-permute-start | bytes 196616 | tf_op jit(solution)/shard_map/ppermute | solution.py:99
  56.5 5.2 %collective-permute-start.21 = (f32[128,128]{1,0:T(8,128)S(1)}, f32[128,128]{1,0:T(8,128)S(1)}, u32[]{:S(2)}, u32[]{:S(2)}) collective-permute-start(f32[128,128]{1,0:T(8,128)S(1)} %shard_map.136.refs_0_), channel_id=1, source_target_pairs={{0,6},{1,25},{2,4},{3,27},{4,2},{5,29},{6,0},{7,31},{8,14},{9,17},... | collective-permute-start | bytes 196616 | tf_op jit(solution)/shard_map/ppermute | solution.py:99
  58.1 4.3 %collective-permute-start.20 = (f32[128,128]{1,0:T(8,128)S(1)}, f32[128,128]{1,0:T(8,128)S(1)}, u32[]{:S(2)}, u32[]{:S(2)}) collective-permute-start(f32[128,128]{1,0:T(8,128)S(1)} %shard_map.136.refs_0_), channel_id=1, source_target_pairs={{0,4},{1,17},{2,6},{3,19},{4,0},{5,21},{6,2},{7,23},{8,12},{9,25},... | collective-permute-start | bytes 196616 | tf_op jit(solution)/shard_map/ppermute | solution.py:99
  59.8 4.3 %collective-permute-start.19 = (f32[128,128]{1,0:T(8,128)S(1)}, f32[128,128]{1,0:T(8,128)S(1)}, u32[]{:S(2)}, u32[]{:S(2)}) collective-permute-start(f32[128,128]{1,0:T(8,128)S(1)} %shard_map.136.refs_0_), channel_id=1, source_target_pairs={{0,2},{1,9},{2,0},{3,11},{4,6},{5,13},{6,4},{7,15},{8,10},{9,1},{1... | collective-permute-start | bytes 196616 | tf_op jit(solution)/shard_map/ppermute | solution.py:99
  64.1 1.9 %collective-permute-start.22 = (f32[64,128]{1,0:T(8,128)S(1)}, f32[64,128]{1,0:T(8,128)S(1)}, u32[]{:S(2)}, u32[]{:S(2)}) collective-permute-start(f32[64,128]{1,0:T(8,128)S(1)} %shard_map.138.refs_0_), channel_id=1, source_target_pairs={{0,1},{1,0},{2,3},{3,2},{4,5},{5,4},{6,7},{7,6},{8,9},{9,8},{10,11... | collective-permute-start | bytes 98312 | tf_op jit(solution)/shard_map/ppermute | solution.py:107
  (7 other events, 19.1 us)

commit v2 on v1

--- a/solution.py
+++ b/solution.py
@@ -29,13 +29,39 @@
 
 
 def dot3(a, b, dims):
-    return raw_dot(a[0], b[0], dims) + (raw_dot(a[0], b[1], dims) + raw_dot(a[1], b[0], dims))
-
-
-def dot_exact(a, b, dims):
-    return lax.dot_general(
-        a, b, (dims, ((), ())), precision=lax.Precision.HIGHEST, preferred_element_type=F32
-    )
+    inner, outer = dims[1][0], 1 - dims[1][0]
+    columns = b[0].shape[outer]
+    depth = b[0].shape[inner]
+    short = depth <= 128
+    left = jnp.concatenate(a, axis=dims[0][0]) if short else a[0]
+    doubled = jnp.concatenate([b[0], b[0]], axis=inner) if short else b[0]
+    if columns <= 128:
+        side = jnp.concatenate([b[1], jnp.zeros_like(b[1])], axis=inner) if short else b[1]
+        first = raw_dot(left, jnp.concatenate([doubled, side], axis=outer), dims)
+        rest = first[:, columns:]
+    else:
+        first = raw_dot(left, doubled, dims)
+        rest = raw_dot(a[0], b[1], dims)
+    if not short:
+        rest = rest + raw_dot(a[1], b[0], dims)
+    return first[:, :columns] + rest
+
+
+def split3(x):
+    high = x.astype(BF16)
+    rest = x - high.astype(F32)
+    middle = rest.astype(BF16)
+    return high, middle, (rest - middle.astype(F32)).astype(BF16)
+
+
+def dot_exact(a, b):
+    (ah, am, al), (bh, bm, bl) = split3(a), split3(b)
+    columns = b.shape[1]
+    stacked = lambda x, y, axis: jnp.concatenate([x, y], axis=axis)
+    square = stacked(stacked(bh, bm, 1), stacked(bm, bh, 1), 0)
+    first = raw_dot(stacked(ah, am, 1), square, NN)
+    rest = raw_dot(stacked(ah, al, 1), stacked(bl, bh, 0), NN)
+    return first[:, :columns] + (first[:, columns:] + rest)
 
 
 def softmaxes(logits):
@@ -138,12 +164,16 @@
     return jax.ShapeDtypeStruct(shape, dtype)
 
 
-def put_message(ref, state, totals):
+def put_rows(ref, state):
     rows, half = state.shape[0], state.shape[1] // 2
     ref[0:rows] = state[:, :half]
     ref[rows : 2 * rows] = state[:, half:]
+
+
+def totals_block(totals):
+    half = totals.shape[1] // 2
     first = lax.broadcasted_iota(jnp.int32, (8, half), 0) < 4
-    ref[2 * rows : 2 * rows + 8] = jnp.where(first, totals[:, :half], totals[:, half:])
+    return jnp.where(first, totals[:, :half], totals[:, half:])
 
 
 def take_totals(piece, rows):
@@ -173,7 +203,7 @@
         copy.start()
     copies[0].wait()
     copies[1].wait()
-    upper, lower = softmaxes(dot_exact(keys[...], weight[...], NN))
+    upper, lower = softmaxes(dot_exact(keys[...], weight[...]))
     feat = split(jnp.concatenate([upper, lower], axis=1))
     feat_high[...] = feat[0]
     feat_low[...] = feat[1]
@@ -182,7 +212,8 @@
     copies[2].wait()
     scratch[...] = dot3(split(values[...]), feat, TN)
     state = scratch[pl.ds(pl.multiple_of(mine * share, 8), share), :]
-    put_message(message, state, totals)
+    put_rows(message, state)
+    message[2 * share :] = totals_block(totals)
 
 
 def causal(size):
@@ -195,7 +226,7 @@
     block, queries, weight, values, key_high, key_low,
     feat_high, feat_low, score_high, score_low, numer, norm,
 ):
-    upper, lower = softmaxes(dot_exact(queries[...], weight[0], NN))
+    upper, lower = softmaxes(dot_exact(queries[...], weight[0]))
     feat = split(jnp.concatenate([upper, lower], axis=1))
     feat_high[...] = feat[0]
     feat_low[...] = feat[1]
@@ -276,66 +307,94 @@
     refs[-1][...] = total
 
 
-def inter_body(heads, peers, share, *refs):
+def carried_body(heads, share, before, scaled, *refs):
+    feats, refs = [refs[2 * h : 2 * h + 2] for h in range(heads)], refs[2 * heads :]
+    locals_, refs = refs[:heads], refs[heads:]
+    norms, refs = refs[:heads], refs[heads:]
+    grads, refs = refs[:heads], refs[heads:]
+    messages, scratch = refs[:-1], refs[-1]
+    mine = lax.axis_index("head")
+    width = grads[0].shape[1]
+    totals = take_totals(before, share)
+    totals = split(jnp.broadcast_to(totals, (width, totals.shape[1])))
+    carried = None
+    for h in range(heads):
+        feat = (feats[h][0][...], feats[h][1][...])
+        norm = locals_[h][...] + dot3(feat, totals, NT)
+        norms[h][...] = norm
+        grad_numer = scaled[:, h * width : (h + 1) * width] / norm
+        grads[h][...] = grad_numer
+        term = dot3(split(grad_numer), feat, TN)
+        carried = term if carried is None else carried + term
+    scratch[...] = carried
+    for m, message in enumerate(messages):
+        put_rows(message, scratch[pl.ds(pl.multiple_of((mine ^ m) * share, 8), share), :])
+
+
+def inter_body(heads, peers, share, scaled, *refs):
     pieces, refs = refs[:peers], refs[peers:]
     feats, refs = [refs[2 * h : 2 * h + 2] for h in range(heads)], refs[2 * heads :]
-    locals_, refs = [refs[2 * h : 2 * h + 2] for h in range(heads)], refs[2 * heads :]
-    scaled, refs = refs[0], refs[1:]
-    state_high, state_low = refs[:2]
-    refs = refs[2:]
-    grads, refs = refs[:heads], refs[heads:]
-    messages, refs = refs[:peers], refs[peers:]
-    scratch, = refs
+    locals_, refs = refs[:heads], refs[heads:]
+    norms, refs = refs[:heads], refs[heads:]
+    state_high, state_low, carried_totals, *refs = refs
+    grads, scratch = refs[:heads], refs[-1]
     mine = lax.axis_index("head")
     for m, piece in enumerate(pieces):
         put_state(piece, scratch, share, mine ^ m)
     state = scratch[...]
     width = state.shape[0]
     totals = jnp.broadcast_to(take_totals(pieces[0], share), state.shape)
-    extended = split(jnp.concatenate([state, totals], axis=0))
-    state_high[...] = extended[0]
-    state_low[...] = extended[1]
+    pair = split(state)
+    state_high[:width] = pair[0]
+    state_low[:width] = pair[1]
+    rest = split(totals)
+    state_high[width:] = rest[0]
+    state_low[width:] = rest[1]
     carried = None
     for h in range(heads):
         feat = (feats[h][0][...], feats[h][1][...])
-        inter = dot3(feat, extended, NT)
-        numer = locals_[h][0][...] + inter[:, :width]
-        norm = locals_[h][1][...] + inter[:, width:]
+        numer = locals_[h][...] + dot3(feat, pair, NT)
+        norm = norms[h][...]
         mine_scaled = scaled[:, h * width : (h + 1) * width]
-        grad_numer = mine_scaled / norm
         along = jnp.sum(mine_scaled * (numer / norm), axis=1, keepdims=True)
-        both = jnp.concatenate([grad_numer, -(along / norm)], axis=1)
-        grads[h][...] = both
-        term = dot3(split(both), feat, TN)
+        grad_norm = -(along / norm)
+        grads[h][...] = grad_norm
+        wide_norm = jnp.concatenate([grad_norm, grad_norm], axis=1)
+        term = jnp.sum(wide_norm * joined(feat), axis=0, keepdims=True)
         carried = term if carried is None else carried + term
-    scratch[...] = carried[:width]
-    for m, message in enumerate(messages):
-        part = scratch[pl.ds(pl.multiple_of((mine ^ m) * share, 8), share), :]
-        put_message(message, part, carried[width : width + 8])
+    carried_totals[...] = totals_block(jnp.broadcast_to(carried, (8, carried.shape[1])))
+
+
+def carried_sum_body(totals, *refs):
+    total = refs[0][...]
+    for piece in refs[1:-1]:
+        total = total + piece[...]
+    rows = total.shape[0]
+    refs[-1][0:rows] = total
+    refs[-1][rows:] = totals[...]
+
+
+def cut(pair, at):
+    return pair[0][at], pair[1][at]
 
 
 def query_grad_body(
-    block, first, queries, values, key_high, key_low, feat_high, feat_low,
-    score_high, score_low, grads, state_high, state_low, *refs,
+    block, queries, values, key_high, key_low, feat_high, feat_low, grad_numer, grad_norm,
+    state_high, state_low, logit_ref, grad_weight, score_grad_high, score_grad_low,
 ):
-    earlier, (logit_ref, grad_weight, grad_key) = refs[:-3], refs[-3:]
     rows, width = values.shape
-    wide = key_high.shape[1]
-    both = grads[...]
-    numer = split(both[:, :width])
-    scale = 1.0 / width
-    extended = split(jnp.concatenate([both[:, :width], both[:, width:] * scale], axis=1))
+    numer = split(grad_numer[...])
+    norm_grad = grad_norm[...]
+    scaled_norm = split(norm_grad * (1.0 / width))
+    extended = [jnp.concatenate([a, b], axis=1) for a, b in zip(numer, scaled_norm)]
     value_pair = split(values[...])
     feat = (feat_high[...], feat_low[...])
     state = (state_high[...], state_low[...])
     mask = causal(block)
-    count = rows // block
-    key_sums, value_sums, logit_parts = [None] * count, [None] * count, []
-    cut = lambda pair, at: (pair[0][at], pair[1][at])
-    for i in range(count):
+    parts = []
+    for i in range(rows // block):
         at = slice(i * block, (i + 1) * block)
-        norm_part = both[at, width:]
-        norm_part = jnp.concatenate([norm_part] * (block // width), axis=1)
+        norm_part = jnp.concatenate([norm_grad[at]] * (block // width), axis=1)
         grad_query = dot3(cut(extended, at), state, NN)
         for j in range(i + 1):
             past = slice(j * block, (j + 1) * block)
@@ -343,24 +402,38 @@
             if i == j:
                 grad_scores = jnp.where(mask, grad_scores, 0.0)
             pair = split(grad_scores)
-            keys = (key_high[past], key_low[past])
-            grad_query = grad_query + dot3(pair, keys, NN)
-            key_term = dot3(pair, cut(feat, at), TN)
-            value_term = dot3((score_high[at, past], score_low[at, past]), cut(numer, at), TN)
-            key_sums[j] = key_term if key_sums[j] is None else key_sums[j] + key_term
-            value_sums[j] = value_term if value_sums[j] is None else value_sums[j] + value_term
-        logit_parts.append(logit_grad(joined(cut(feat, at)), grad_query))
-    grad_logits = jnp.concatenate(logit_parts, axis=0)
+            score_grad_high[at, past] = pair[0]
+            score_grad_low[at, past] = pair[1]
+            grad_query = grad_query + dot3(pair, (key_high[past], key_low[past]), NN)
+        parts.append(logit_grad(joined(cut(feat, at)), grad_query))
+    grad_logits = jnp.concatenate(parts, axis=0)
     logit_ref[...] = grad_logits
     grad_weight[...] = dot3(split(queries[...]), split(grad_logits), TN)
+
+
+def key_inner_body(block, heads, *refs):
+    result = refs[-1]
+    rows, wide = refs[0].shape
+    count = rows // block
+    key_sums, value_sums = [None] * count, [None] * count
+    for h in range(heads):
+        *pairs, grads = refs[7 * h : 7 * h + 7]
+        feat, scores, score_grads = pairs[0:2], pairs[2:4], pairs[4:6]
+        numer = split(grads[...])
+        for i in range(count):
+            at = slice(i * block, (i + 1) * block)
+            for j in range(i + 1):
+                past = slice(j * block, (j + 1) * block)
+                pair = (score_grads[0][at, past], score_grads[1][at, past])
+                term = dot3(pair, cut(feat, at), TN)
+                key_sums[j] = term if key_sums[j] is None else key_sums[j] + term
+                pair = (scores[0][at, past], scores[1][at, past])
+                term = dot3(pair, cut(numer, at), TN)
+                value_sums[j] = term if value_sums[j] is None else value_sums[j] + term
     for j in range(count):
         past = slice(j * block, (j + 1) * block)
-        if first:
-            grad_key[past, :wide] = key_sums[j]
-            grad_key[past, wide:] = value_sums[j]
-        else:
-            grad_key[past, :wide] = earlier[0][past, :wide] + key_sums[j]
-            grad_key[past, wide:] = earlier[0][past, wide:] + value_sums[j]
+        result[past, :wide] = key_sums[j]
+        result[past, wide:] = value_sums[j]
 
 
 def query_out_body(heads, weights, *refs):
@@ -387,7 +460,7 @@
     state = split(scratch[...])
     state_high[...] = state[0]
     state_low[...] = state[1]
-    totals = jnp.where(mine == 0, take_totals(piece, share), 0.0)
+    totals = take_totals(piece, share)
     wide = key_high.shape[1]
     grad = dot3(split(values[...]), state, NN) + totals + inner[:, :wide]
     feat = (key_high[...], key_low[...])
@@ -553,41 +626,52 @@
         scores.append(results[2:4])
         inner.append(results[4:6])
 
+    flat_feats = [x for pair in feats for x in pair]
+    results = call(
+        bind(carried_body, heads, share),
+        [out((rows, width))] * (2 * heads) + [out((2 * share, half))] * peers,
+        (before, scaled, *flat_feats, *[pair[1] for pair in inner]),
+        6 * heads * unit,
+        scratch=[pltpu.VMEM((width, wide), F32)],
+    )
+    norms, results = results[:heads], results[heads:]
+    grads, results = results[:heads], results[heads:]
+    carried_parts = [results[0]] + exchange(results[1:], peers)
     results = call(
         bind(inter_body, heads, peers, share),
         [out((2 * width, wide), BF16)] * 2
-        + [out((rows, 2 * width))] * heads
-        + [out(message)] * peers,
-        (
-            *prefix,
-            *[x for pair in feats for x in pair],
-            *[x for pair in inner for x in pair],
-            scaled,
-        ),
-        12 * heads * unit,
+        + [out((8, half))]
+        + [out((rows, width))] * heads,
+        (scaled, *prefix, *flat_feats, *[pair[0] for pair in inner], *norms),
+        4 * heads * unit,
         scratch=[pltpu.VMEM((width, wide), F32)],
     )
-    state, results = results[:2], results[2:]
-    grads, results = results[:heads], results[heads:]
-    sends = exchange(results[1:], peers)
-    (carried,) = call(sum_body, [out(message)], (results[0], *sends))
-
-    weight_grads, query_logits, key_inner = [], [], None
+    state, carried_totals, norm_grads = results[:2], results[2], results[3:]
+    (carried,) = call(carried_sum_body, [out(message)], (carried_totals, *carried_parts))
+
+    weight_grads, query_logits, inner_args = [], [], []
     for h in range(heads):
-        args = [queries, values, key_high, key_low, *feats[h], *scores[h], grads[h], *state]
-        outs = [out((rows, half)), out((width, half)), out((rows, wide + width))]
-        if h > 0:
-            args.append(key_inner)
-        logits, grad_weight, key_inner = call(
-            bind(query_grad_body, block, h == 0),
+        args = [
+            queries, values, key_high, key_low, *feats[h], grads[h], norm_grads[h], *state,
+        ]
+        outs = [out((rows, half)), out((width, half))] + [out((rows, rows), BF16)] * 2
+        logits, grad_weight, *score_grads = call(
+            bind(query_grad_body, block),
             outs,
             args,
-            14 * unit,
+            8 * unit,
             [query_spec(h)] + [whole(a.shape) for a in args[1:]],
             [whole(o.shape) for o in outs],
         )
         query_logits.append(logits)
         weight_grads.append(grad_weight)
+        inner_args += [*feats[h], *scores[h], *score_grads, grads[h]]
+    (key_inner,) = call(
+        bind(key_inner_body, block, heads),
+        [out((rows, wide + width))],
+        inner_args,
+        6 * heads * unit,
+    )
     (grad_queries,) = call(
         bind(query_out_body, heads),
         [out((rows, heads * width))],

time: 67.6 us -> 61.6 us (0.911)
  waiting for transfers between devices: 23.5 us -> 17.7 us
    ppermute x18, waiting for transfers between devices: 21.2 us -> 16.3 us  [swap(): received.append(lax.ppermute(value, ('ctx', 'head'), pairs))]
    ppermute x5, waiting for transfers between devices: 2.31 us -> 1.33 us  [exchange(): lax.ppermute(value, 'head', [(i, i ^ m) for i in range(peers)])]
    pallas_call x21 -> x23, Pallas kernels: 16 us -> 15.4 us  [call(): pl.pallas_call(body, out_shape=outs, scratch_shapes=scratch, cost_estimat...]
  transfers between devices with their start and end apart: 23 -> 23, of which waited for: 15 -> 14; matrix products, arithmetic and copies ran while one was open for 0% -> 0% of each run, Pallas kernels for 14% -> 18%
where the time goes in v2:
time: 61.6 us; the launch traced here: 61.4 us
  starting transfers between devices  26.4 us (43%)
  waiting for transfers between devices  17.7 us (29%)
  Pallas kernels  15.4 us (25%)
  local copies, waits for them, and re-layouts  0.93 us (2%)
  between operations  0.87 us (1%)
    ppermute x18, starting transfers between devices, swap(): received.append(lax.ppermute(value, ('ctx', 'head'), pairs))  25.1 us
    ppermute x18, waiting for transfers between devices, swap(): received.append(lax.ppermute(value, ('ctx', 'head'), pairs))  16.3 us
    pallas_call x23, Pallas kernels, call(): pl.pallas_call(body, out_shape=outs, scratch_shapes=scratch, cost_estimat...  15.4 us
    ppermute x5, waiting for transfers between devices, exchange(): lax.ppermute(value, 'head', [(i, i ^ m) for i in range(peers)])  1.33 us
    ppermute x5, starting transfers between devices, exchange(): lax.ppermute(value, 'head', [(i, i ^ m) for i in range(peers)])  1.27 us
  transfers between devices with their start and end apart: 23, of which 14 were waited for; matrix products, arithmetic and copies ran while one was open for 0% of the time, Pallas kernels for 18%

profile of v2, /device:TPU:0, one launch (start us, length us, event | category | flops | bytes accessed | tf_op | source)
XLA Modules:
  0.0 61.4 jit_solution(13774922401259281349)
XLA Ops:
  0.7 2.2 %shard_map.119 = (bf16[512,256]{1,0:T(8,128)(2,1)S(1)}, bf16[512,256]{1,0:T(8,128)(2,1)S(1)}, f32[136,128]{1,0:T(8,128)S(1)}) custom-call(f32[512,128]{1,0:T(8,128)} %keys.1, f32[512,128]{1,0:T(8,128)} %values.9, f32[128,128]{1,0:T(8,128)} %weight.5), custom_call_target="tpu_custom_call" | custom-call | flops 201326592 | bytes 1708032 | tf_op jit(solution)/shard_map/pallas_call | solution.py:149
  2.9 4.0 %collective-permute-start.2 = (f32[136,128]{1,0:T(8,128)S(1)}, f32[136,128]{1,0:T(8,128)S(1)}, u32[]{:S(2)}, u32[]{:S(2)}) collective-permute-start(f32[136,128]{1,0:T(8,128)S(1)} %get-tuple-element.61.local), channel_id=1, source_target_pairs={{0,6},{1,25},{2,4},{3,27},{4,2},{5,29},{6,0},{7,31},{8,14},{9,17},... | collective-permute-start | bytes 208904 | tf_op jit(solution)/shard_map/ppermute | solution.py:125
  7.6 1.5 %collective-permute-done.2.refs_2_ = f32[136,128]{1,0:T(8,128)S(1)} collective-permute-done((f32[136,128]{1,0:T(8,128)S(1)}, f32[136,128]{1,0:T(8,128)S(1)}, u32[]{:S(2)}, u32[]{:S(2)}) %collective-permute-start.2) | collective-permute-done | bytes 69664 | tf_op jit(solution)/shard_map/ppermute | solution.py:125
  9.2 2.0 %collective-permute-done.1.refs_1_ = f32[136,128]{1,0:T(8,128)S(1)} collective-permute-done((f32[136,128]{1,0:T(8,128)S(1)}, f32[136,128]{1,0:T(8,128)S(1)}, u32[]{:S(2)}, u32[]{:S(2)}) %collective-permute-start.1) | collective-permute-done | bytes 69664 | tf_op jit(solution)/shard_map/ppermute | solution.py:125
  11.8 1.6 %collective-permute-start.3 = (f32[136,128]{1,0:T(8,128)S(1)}, f32[136,128]{1,0:T(8,128)S(1)}, u32[]{:S(2)}, u32[]{:S(2)}) collective-permute-start(f32[136,128]{1,0:T(8,128)S(1)} %get-tuple-element.63), channel_id=1, source_target_pairs={{0,8},{1,3},{2,10},{3,1},{4,12},{5,7},{6,14},{7,5},{8,0},{9,11},{1... | collective-permute-start | bytes 208904 | tf_op jit(solution)/shard_map/ppermute | solution.py:125
  13.4 2.6 %collective-permute-start.4 = (f32[136,128]{1,0:T(8,128)S(1)}, f32[136,128]{1,0:T(8,128)S(1)}, u32[]{:S(2)}, u32[]{:S(2)}) collective-permute-start(f32[136,128]{1,0:T(8,128)S(1)} %get-tuple-element.64), channel_id=1, source_target_pairs={{0,16},{1,5},{2,18},{3,7},{4,20},{5,1},{6,22},{7,3},{8,24},{9,13},... | collective-permute-start | bytes 208904 | tf_op jit(solution)/shard_map/ppermute | solution.py:125
  17.1 1.3 %shard_map.123 = (bf16[512,256]{1,0:T(8,128)(2,1)S(1)}, bf16[512,256]{1,0:T(8,128)(2,1)S(1)}, bf16[512,512]{1,0:T(8,128)(2,1)S(1)}, bf16[512,512]{1,0:T(8,128)(2...) custom-call(f32[512,256]{1,0:T(8,128)S(1)} %copy-done, f32[2,128,128]{2,1,0:T(8,128)S(1)} %copy-done.2, ...), custom_call_target="tpu_custom_call" | custom-call | flops 301989888 | bytes 5636096 | tf_op jit(solution)/shard_map/pallas_call | solution.py:149
  18.5 1.3 %shard_map.120 = (bf16[512,256]{1,0:T(8,128)(2,1)S(1)}, bf16[512,256]{1,0:T(8,128)(2,1)S(1)}, bf16[512,512]{1,0:T(8,128)(2,1)S(1)}, bf16[512,512]{1,0:T(8,128)(2...) custom-call(f32[512,256]{1,0:T(8,128)S(1)} %copy-done, f32[2,128,128]{2,1,0:T(8,128)S(1)} %copy-done.2, ...), custom_call_target="tpu_custom_call" | custom-call | flops 301989888 | bytes 5636096 | tf_op jit(solution)/shard_map/pallas_call | solution.py:149
  19.9 2.2 %collective-permute-done.5.refs_2_ = f32[136,128]{1,0:T(8,128)S(1)} collective-permute-done((f32[136,128]{1,0:T(8,128)S(1)}, f32[136,128]{1,0:T(8,128)S(1)}, u32[]{:S(2)}, u32[]{:S(2)}) %collective-permute-start.5) | collective-permute-done | bytes 69664 | tf_op jit(solution)/shard_map/ppermute | solution.py:125
  25.7 3.5 %collective-permute-start.8 = (f32[136,128]{1,0:T(8,128)S(1)}, f32[136,128]{1,0:T(8,128)S(1)}, u32[]{:S(2)}, u32[]{:S(2)}) collective-permute-start(f32[136,128]{1,0:T(8,128)S(1)} %shard_map.129.local), channel_id=1, source_target_pairs={{0,8},{1,3},{2,10},{3,1},{4,12},{5,7},{6,14},{7,5},{8,0},{9,11},{1... | collective-permute-start | bytes 208904 | tf_op jit(solution)/shard_map/ppermute | solution.py:125
  29.3 1.5 %shard_map.126 = (f32[512,128]{1,0:T(8,128)S(1)}, f32[128,128]{1,0:T(8,128)S(1)}, bf16[512,512]{1,0:T(8,128)(2,1)S(1)}, bf16[512,512]{1,0:T(8,128)(2,1)S(1)}) custom-call(f32[512,256]{1,0:T(8,128)S(1)} %copy-done, f32[512,128]{1,0:T(8,128)S(1)} %copy-done.1, bf16[512,256]{1,0:T(8,128)(2,1)S(1)} %get-tuple-element.57.key_high, ...), custom_call_target="tpu_custom_call" | custom-call | flops 268435456 | bytes 6356992 | tf_op jit(solution)/shard_map/pallas_call | solution.py:149
  30.8 1.5 %shard_map.127 = (f32[512,128]{1,0:T(8,128)S(1)}, f32[128,128]{1,0:T(8,128)S(1)}, bf16[512,512]{1,0:T(8,128)(2,1)S(1)}, bf16[512,512]{1,0:T(8,128)(2,1)S(1)}) custom-call(f32[512,256]{1,0:T(8,128)S(1)} %copy-done, f32[512,128]{1,0:T(8,128)S(1)} %copy-done.1, bf16[512,256]{1,0:T(8,128)(2,1)S(1)} %get-tuple-element.57.key_high, ...), custom_call_target="tpu_custom_call" | custom-call | flops 268435456 | bytes 6356992 | tf_op jit(solution)/shard_map/pallas_call | solution.py:149
  33.1 1.5 %collective-permute-start.12 = (f32[200,128]{1,0:T(8,128)S(1)}, f32[200,128]{1,0:T(8,128)S(1)}, u32[]{:S(2)}, u32[]{:S(2)}) collective-permute-start(f32[200,128]{1,0:T(8,128)S(1)} %get-tuple-element.89), channel_id=1, source_target_pairs={{0,4},{1,17},{2,6},{3,19},{4,0},{5,21},{6,2},{7,23},{8,12},{9,25},... | collective-permute-start | bytes 307208 | tf_op jit(solution)/shard_map/ppermute | solution.py:125
  34.6 1.4 %collective-permute-start.13 = (f32[200,128]{1,0:T(8,128)S(1)}, f32[200,128]{1,0:T(8,128)S(1)}, u32[]{:S(2)}, u32[]{:S(2)}) collective-permute-start(f32[200,128]{1,0:T(8,128)S(1)} %get-tuple-element.90), channel_id=1, source_target_pairs={{0,6},{1,25},{2,4},{3,27},{4,2},{5,29},{6,0},{7,31},{8,14},{9,17},... | collective-permute-start | bytes 307208 | tf_op jit(solution)/shard_map/ppermute | solution.py:125
  36.1 1.2 %shard_map.132.inner = f32[512,384]{1,0:T(8,128)S(1)} custom-call(bf16[512,256]{1,0:T(8,128)(2,1)S(1)} %get-tuple-element.59.refs_0_.refs_2_.feat_high, bf16[512,256]{1,0:T(8,128)(2,1)S(1)} %get-tuple-element.60.refs_1_.refs_3_.feat_low, bf16[512,512]{1,0:T(8,128)(2,1)S(1)} %get-tuple-element.91.refs_2_, bf16[512,512]{1,0:T(8,128)(2,1)S(1)} %get-tuple-element.92.refs_3_, ...), custom_call_target="tpu_custom_call" | custom-call | flops 402653184 | bytes 11796480 | tf_op jit(solution)/shard_map/pallas_call | solution.py:149
  37.8 2.4 %collective-permute-done.13.refs_2_ = f32[200,128]{1,0:T(8,128)S(1)} collective-permute-done((f32[200,128]{1,0:T(8,128)S(1)}, f32[200,128]{1,0:T(8,128)S(1)}, u32[]{:S(2)}, u32[]{:S(2)}) %collective-permute-start.13) | collective-permute-done | bytes 102432 | tf_op jit(solution)/shard_map/ppermute | solution.py:125
  43.2 1.6 %collective-permute-start.18 = (f32[128,128]{1,0:T(8,128)S(1)}, f32[128,128]{1,0:T(8,128)S(1)}, u32[]{:S(2)}, u32[]{:S(2)}) collective-permute-start(f32[128,128]{1,0:T(8,128)S(1)} %shard_map.137.refs_0_), channel_id=1, source_target_pairs={{0,24},{1,7},{2,26},{3,5},{4,28},{5,3},{6,30},{7,1},{8,16},{9,15},... | collective-permute-start | bytes 196616 | tf_op jit(solution)/shard_map/ppermute | solution.py:125
  45.9 1.8 %collective-permute-start.16 = (f32[128,128]{1,0:T(8,128)S(1)}, f32[128,128]{1,0:T(8,128)S(1)}, u32[]{:S(2)}, u32[]{:S(2)}) collective-permute-start(f32[128,128]{1,0:T(8,128)S(1)} %shard_map.137.refs_0_), channel_id=1, source_target_pairs={{0,8},{1,3},{2,10},{3,1},{4,12},{5,7},{6,14},{7,5},{8,0},{9,11},{1... | collective-permute-start | bytes 196616 | tf_op jit(solution)/shard_map/ppermute | solution.py:125
  47.7 1.7 %collective-permute-done.18.refs_3_ = f32[128,128]{1,0:T(8,128)S(1)} collective-permute-done((f32[128,128]{1,0:T(8,128)S(1)}, f32[128,128]{1,0:T(8,128)S(1)}, u32[]{:S(2)}, u32[]{:S(2)}) %collective-permute-start.18) | collective-permute-done | bytes 65568 | tf_op jit(solution)/shard_map/ppermute | solution.py:125
  49.4 1.5 %collective-permute-done.17.refs_2_ = f32[128,128]{1,0:T(8,128)S(1)} collective-permute-done((f32[128,128]{1,0:T(8,128)S(1)}, f32[128,128]{1,0:T(8,128)S(1)}, u32[]{:S(2)}, u32[]{:S(2)}) %collective-permute-start.17) | collective-permute-done | bytes 65568 | tf_op jit(solution)/shard_map/ppermute | solution.py:125
  50.9 1.5 %collective-permute-start.21 = (f32[128,128]{1,0:T(8,128)S(1)}, f32[128,128]{1,0:T(8,128)S(1)}, u32[]{:S(2)}, u32[]{:S(2)}) collective-permute-start(f32[128,128]{1,0:T(8,128)S(1)} %shard_map.138.refs_0_), channel_id=1, source_target_pairs={{0,6},{1,25},{2,4},{3,27},{4,2},{5,29},{6,0},{7,31},{8,14},{9,17},... | collective-permute-start | bytes 196616 | tf_op jit(solution)/shard_map/ppermute | solution.py:125
  52.4 1.5 %collective-permute-start.20 = (f32[128,128]{1,0:T(8,128)S(1)}, f32[128,128]{1,0:T(8,128)S(1)}, u32[]{:S(2)}, u32[]{:S(2)}) collective-permute-start(f32[128,128]{1,0:T(8,128)S(1)} %shard_map.138.refs_0_), channel_id=1, source_target_pairs={{0,4},{1,17},{2,6},{3,19},{4,0},{5,21},{6,2},{7,23},{8,12},{9,25},... | collective-permute-start | bytes 196616 | tf_op jit(solution)/shard_map/ppermute | solution.py:125
  54.4 1.7 %collective-permute-done.21.refs_3_ = f32[128,128]{1,0:T(8,128)S(1)} collective-permute-done((f32[128,128]{1,0:T(8,128)S(1)}, f32[128,128]{1,0:T(8,128)S(1)}, u32[]{:S(2)}, u32[]{:S(2)}) %collective-permute-start.21) | collective-permute-done | bytes 65568 | tf_op jit(solution)/shard_map/ppermute | solution.py:125
  56.8 1.4 %collective-permute-done.19.refs_1_ = f32[128,128]{1,0:T(8,128)S(1)} collective-permute-done((f32[128,128]{1,0:T(8,128)S(1)}, f32[128,128]{1,0:T(8,128)S(1)}, u32[]{:S(2)}, u32[]{:S(2)}) %collective-permute-start.19) | collective-permute-done | bytes 65568 | tf_op jit(solution)/shard_map/ppermute | solution.py:125
  (63 shorter events, 16.0 us)
Async XLA Ops:
  0.6 15.6 %copy-start.5 = (f32[512,256]{1,0:T(8,128)S(1)}, f32[512,256]{1,0:T(8,128)}, u32[]{:S(2)}) copy-start(f32[512,256]{1,0:T(8,128)} %param.11) | copy-start | bytes 1572868
  2.9 6.3 %collective-permute-start.2 = (f32[136,128]{1,0:T(8,128)S(1)}, f32[136,128]{1,0:T(8,128)S(1)}, u32[]{:S(2)}, u32[]{:S(2)}) collective-permute-start(f32[136,128]{1,0:T(8,128)S(1)} %get-tuple-element.61.local), channel_id=1, source_target_pairs={{0,6},{1,25},{2,4},{3,27},{4,2},{5,29},{6,0},{7,31},{8,14},{9,17},... | collective-permute-start | bytes 208904 | tf_op jit(solution)/shard_map/ppermute | solution.py:125
  6.9 4.3 %collective-permute-start.1 = (f32[136,128]{1,0:T(8,128)S(1)}, f32[136,128]{1,0:T(8,128)S(1)}, u32[]{:S(2)}, u32[]{:S(2)}) collective-permute-start(f32[136,128]{1,0:T(8,128)S(1)} %get-tuple-element.61.local), channel_id=1, source_target_pairs={{0,4},{1,17},{2,6},{3,19},{4,0},{5,21},{6,2},{7,23},{8,12},{9,25},... | collective-permute-start | bytes 208904 | tf_op jit(solution)/shard_map/ppermute | solution.py:125
  7.4 4.3 %collective-permute-start = (f32[136,128]{1,0:T(8,128)S(1)}, f32[136,128]{1,0:T(8,128)S(1)}, u32[]{:S(2)}, u32[]{:S(2)}) collective-permute-start(f32[136,128]{1,0:T(8,128)S(1)} %get-tuple-element.61.local), channel_id=1, source_target_pairs={{0,2},{1,9},{2,0},{3,11},{4,6},{5,13},{6,4},{7,15},{8,10},{9,1},{1... | collective-permute-start | bytes 208904 | tf_op jit(solution)/shard_map/ppermute | solution.py:125
  11.8 8.1 %collective-permute-start.3 = (f32[136,128]{1,0:T(8,128)S(1)}, f32[136,128]{1,0:T(8,128)S(1)}, u32[]{:S(2)}, u32[]{:S(2)}) collective-permute-start(f32[136,128]{1,0:T(8,128)S(1)} %get-tuple-element.63), channel_id=1, source_target_pairs={{0,8},{1,3},{2,10},{3,1},{4,12},{5,7},{6,14},{7,5},{8,0},{9,11},{1... | collective-permute-start | bytes 208904 | tf_op jit(solution)/shard_map/ppermute | solution.py:125
  13.4 6.4 %collective-permute-start.4 = (f32[136,128]{1,0:T(8,128)S(1)}, f32[136,128]{1,0:T(8,128)S(1)}, u32[]{:S(2)}, u32[]{:S(2)}) collective-permute-start(f32[136,128]{1,0:T(8,128)S(1)} %get-tuple-element.64), channel_id=1, source_target_pairs={{0,16},{1,5},{2,18},{3,7},{4,20},{5,1},{6,22},{7,3},{8,24},{9,13},... | collective-permute-start | bytes 208904 | tf_op jit(solution)/shard_map/ppermute | solution.py:125
  16.0 6.1 %collective-permute-start.5 = (f32[136,128]{1,0:T(8,128)S(1)}, f32[136,128]{1,0:T(8,128)S(1)}, u32[]{:S(2)}, u32[]{:S(2)}) collective-permute-start(f32[136,128]{1,0:T(8,128)S(1)} %get-tuple-element.65), channel_id=1, source_target_pairs={{0,24},{1,7},{2,26},{3,5},{4,28},{5,3},{6,30},{7,1},{8,16},{9,15},... | collective-permute-start | bytes 208904 | tf_op jit(solution)/shard_map/ppermute | solution.py:125
  22.1 1.8 %collective-permute-start.6 = (f32[136,128]{1,0:T(8,128)S(1)}, f32[136,128]{1,0:T(8,128)S(1)}, u32[]{:S(2)}, u32[]{:S(2)}) collective-permute-start(f32[136,128]{1,0:T(8,128)S(1)} %shard_map.122.before.refs_0_), channel_id=1, source_target_pairs={{0,1},{1,0},{2,3},{3,2},{4,5},{5,4},{6,7},{7,6},{8,9},{9,8},{10,11... | collective-permute-start | bytes 208904 | tf_op jit(solution)/shard_map/ppermute | solution.py:133
  23.3 1.5 %collective-permute-start.7 = (f32[128,128]{1,0:T(8,128)S(1)}, f32[128,128]{1,0:T(8,128)S(1)}, u32[]{:S(2)}, u32[]{:S(2)}) collective-permute-start(f32[128,128]{1,0:T(8,128)S(1)} %get-tuple-element.84), channel_id=1, source_target_pairs={{0,1},{1,0},{2,3},{3,2},{4,5},{5,4},{6,7},{7,6},{8,9},{9,8},{10,11... | collective-permute-start | bytes 196616 | tf_op jit(solution)/shard_map/ppermute | solution.py:133
  24.8 7.4 %collective-permute-start.10 = (f32[136,128]{1,0:T(8,128)S(1)}, f32[136,128]{1,0:T(8,128)S(1)}, u32[]{:S(2)}, u32[]{:S(2)}) collective-permute-start(f32[136,128]{1,0:T(8,128)S(1)} %shard_map.129.local), channel_id=1, source_target_pairs={{0,24},{1,7},{2,26},{3,5},{4,28},{5,3},{6,30},{7,1},{8,16},{9,15},... | collective-permute-start | bytes 208904 | tf_op jit(solution)/shard_map/ppermute | solution.py:125
  25.7 6.7 %collective-permute-start.9 = (f32[136,128]{1,0:T(8,128)S(1)}, f32[136,128]{1,0:T(8,128)S(1)}, u32[]{:S(2)}, u32[]{:S(2)}) collective-permute-start(f32[136,128]{1,0:T(8,128)S(1)} %shard_map.129.local), channel_id=1, source_target_pairs={{0,16},{1,5},{2,18},{3,7},{4,20},{5,1},{6,22},{7,3},{8,24},{9,13},... | collective-permute-start | bytes 208904 | tf_op jit(solution)/shard_map/ppermute | solution.py:125
  25.7 6.7 %collective-permute-start.8 = (f32[136,128]{1,0:T(8,128)S(1)}, f32[136,128]{1,0:T(8,128)S(1)}, u32[]{:S(2)}, u32[]{:S(2)}) collective-permute-start(f32[136,128]{1,0:T(8,128)S(1)} %shard_map.129.local), channel_id=1, source_target_pairs={{0,8},{1,3},{2,10},{3,1},{4,12},{5,7},{6,14},{7,5},{8,0},{9,11},{1... | collective-permute-start | bytes 208904 | tf_op jit(solution)/shard_map/ppermute | solution.py:125
  32.5 4.8 %collective-permute-start.11 = (f32[200,128]{1,0:T(8,128)S(1)}, f32[200,128]{1,0:T(8,128)S(1)}, u32[]{:S(2)}, u32[]{:S(2)}) collective-permute-start(f32[200,128]{1,0:T(8,128)S(1)} %get-tuple-element.88), channel_id=1, source_target_pairs={{0,2},{1,9},{2,0},{3,11},{4,6},{5,13},{6,4},{7,15},{8,10},{9,1},{1... | collective-permute-start | bytes 307208 | tf_op jit(solution)/shard_map/ppermute | solution.py:125
  33.1 4.7 %collective-permute-start.12 = (f32[200,128]{1,0:T(8,128)S(1)}, f32[200,128]{1,0:T(8,128)S(1)}, u32[]{:S(2)}, u32[]{:S(2)}) collective-permute-start(f32[200,128]{1,0:T(8,128)S(1)} %get-tuple-element.89), channel_id=1, source_target_pairs={{0,4},{1,17},{2,6},{3,19},{4,0},{5,21},{6,2},{7,23},{8,12},{9,25},... | collective-permute-start | bytes 307208 | tf_op jit(solution)/shard_map/ppermute | solution.py:125
  34.6 5.6 %collective-permute-start.13 = (f32[200,128]{1,0:T(8,128)S(1)}, f32[200,128]{1,0:T(8,128)S(1)}, u32[]{:S(2)}, u32[]{:S(2)}) collective-permute-start(f32[200,128]{1,0:T(8,128)S(1)} %get-tuple-element.90), channel_id=1, source_target_pairs={{0,6},{1,25},{2,4},{3,27},{4,2},{5,29},{6,0},{7,31},{8,14},{9,17},... | collective-permute-start | bytes 307208 | tf_op jit(solution)/shard_map/ppermute | solution.py:125
  41.6 19.1 %collective-permute-start.14 = (f32[256,256]{1,0:T(8,128)S(1)}, f32[256,256]{1,0:T(8,128)S(1)}, u32[]{:S(2)}, u32[]{:S(2)}) collective-permute-start(f32[256,256]{1,0:T(8,128)S(1)} %get-tuple-element.103), channel_id=1, source_target_pairs={{0,1},{1,0},{2,3},{3,2},{4,5},{5,4},{6,7},{7,6},{8,9},{9,8},{10,11... | collective-permute-start | bytes 786440 | tf_op jit(solution)/shard_map/ppermute | solution.py:133
  41.6 1.6 %collective-permute-start.15 = (f32[64,128]{1,0:T(8,128)S(1)}, f32[64,128]{1,0:T(8,128)S(1)}, u32[]{:S(2)}, u32[]{:S(2)}) collective-permute-start(f32[64,128]{1,0:T(8,128)S(1)} %get-tuple-element.107), channel_id=1, source_target_pairs={{0,1},{1,0},{2,3},{3,2},{4,5},{5,4},{6,7},{7,6},{8,9},{9,8},{10,11... | collective-permute-start | bytes 98312 | tf_op jit(solution)/shard_map/ppermute | solution.py:133
  43.2 6.1 %collective-permute-start.18 = (f32[128,128]{1,0:T(8,128)S(1)}, f32[128,128]{1,0:T(8,128)S(1)}, u32[]{:S(2)}, u32[]{:S(2)}) collective-permute-start(f32[128,128]{1,0:T(8,128)S(1)} %shard_map.137.refs_0_), channel_id=1, source_target_pairs={{0,24},{1,7},{2,26},{3,5},{4,28},{5,3},{6,30},{7,1},{8,16},{9,15},... | collective-permute-start | bytes 196616 | tf_op jit(solution)/shard_map/ppermute | solution.py:125
  44.8 6.1 %collective-permute-start.17 = (f32[128,128]{1,0:T(8,128)S(1)}, f32[128,128]{1,0:T(8,128)S(1)}, u32[]{:S(2)}, u32[]{:S(2)}) collective-permute-start(f32[128,128]{1,0:T(8,128)S(1)} %shard_map.137.refs_0_), channel_id=1, source_target_pairs={{0,16},{1,5},{2,18},{3,7},{4,20},{5,1},{6,22},{7,3},{8,24},{9,13},... | collective-permute-start | bytes 196616 | tf_op jit(solution)/shard_map/ppermute | solution.py:125
  45.9 5.0 %collective-permute-start.16 = (f32[128,128]{1,0:T(8,128)S(1)}, f32[128,128]{1,0:T(8,128)S(1)}, u32[]{:S(2)}, u32[]{:S(2)}) collective-permute-start(f32[128,128]{1,0:T(8,128)S(1)} %shard_map.137.refs_0_), channel_id=1, source_target_pairs={{0,8},{1,3},{2,10},{3,1},{4,12},{5,7},{6,14},{7,5},{8,0},{9,11},{1... | collective-permute-start | bytes 196616 | tf_op jit(solution)/shard_map/ppermute | solution.py:125
  50.9 5.2 %collective-permute-start.21 = (f32[128,128]{1,0:T(8,128)S(1)}, f32[128,128]{1,0:T(8,128)S(1)}, u32[]{:S(2)}, u32[]{:S(2)}) collective-permute-start(f32[128,128]{1,0:T(8,128)S(1)} %shard_map.138.refs_0_), channel_id=1, source_target_pairs={{0,6},{1,25},{2,4},{3,27},{4,2},{5,29},{6,0},{7,31},{8,14},{9,17},... | collective-permute-start | bytes 196616 | tf_op jit(solution)/shard_map/ppermute | solution.py:125
  52.4 4.4 %collective-permute-start.20 = (f32[128,128]{1,0:T(8,128)S(1)}, f32[128,128]{1,0:T(8,128)S(1)}, u32[]{:S(2)}, u32[]{:S(2)}) collective-permute-start(f32[128,128]{1,0:T(8,128)S(1)} %shard_map.138.refs_0_), channel_id=1, source_target_pairs={{0,4},{1,17},{2,6},{3,19},{4,0},{5,21},{6,2},{7,23},{8,12},{9,25},... | collective-permute-start | bytes 196616 | tf_op jit(solution)/shard_map/ppermute | solution.py:125
  53.9 4.3 %collective-permute-start.19 = (f32[128,128]{1,0:T(8,128)S(1)}, f32[128,128]{1,0:T(8,128)S(1)}, u32[]{:S(2)}, u32[]{:S(2)}) collective-permute-start(f32[128,128]{1,0:T(8,128)S(1)} %shard_map.138.refs_0_), channel_id=1, source_target_pairs={{0,2},{1,9},{2,0},{3,11},{4,6},{5,13},{6,4},{7,15},{8,10},{9,1},{1... | collective-permute-start | bytes 196616 | tf_op jit(solution)/shard_map/ppermute | solution.py:125
  58.2 1.9 %collective-permute-start.22 = (f32[64,128]{1,0:T(8,128)S(1)}, f32[64,128]{1,0:T(8,128)S(1)}, u32[]{:S(2)}, u32[]{:S(2)}) collective-permute-start(f32[64,128]{1,0:T(8,128)S(1)} %shard_map.140.refs_0_), channel_id=1, source_target_pairs={{0,1},{1,0},{2,3},{3,2},{4,5},{5,4},{6,7},{7,6},{8,9},{9,8},{10,11... | collective-permute-start | bytes 98312 | tf_op jit(solution)/shard_map/ppermute | solution.py:133
  (7 other events, 18.6 us)

commit v3 on v2

--- a/solution.py
+++ b/solution.py
@@ -47,6 +47,11 @@
     return first[:, :columns] + rest
 
 
+def dot5(a, b, dims):
+    small = raw_dot(a[1], b[1], dims) + raw_dot(a[0], b[2], dims)
+    return dot3(a, b[:2], dims) + small
+
+
 def split3(x):
     high = x.astype(BF16)
     rest = x - high.astype(F32)
@@ -190,8 +195,8 @@
 
 
 def key_body(
-    share, keys_hbm, values_hbm, weight_hbm, feat_high, feat_low, message,
-    scratch, keys, values, weight, arrived,
+    share, keys_hbm, values_hbm, weight_hbm, feat_high, feat_low, feat_rest,
+    message, scratch, keys, values, weight, arrived,
 ):
     mine = lax.axis_index("head")
     pairs = [(keys_hbm, keys), (weight_hbm, weight), (values_hbm, values)]
@@ -204,7 +209,9 @@
     copies[0].wait()
     copies[1].wait()
     upper, lower = softmaxes(dot_exact(keys[...], weight[...]))
-    feat = split(jnp.concatenate([upper, lower], axis=1))
+    feat = split3(jnp.concatenate([upper, lower], axis=1))
+    feat_rest[...] = feat[2]
+    feat = feat[:2]
     feat_high[...] = feat[0]
     feat_low[...] = feat[1]
     ones = jnp.ones((8, feat[0].shape[0]), BF16)
@@ -336,7 +343,7 @@
     feats, refs = [refs[2 * h : 2 * h + 2] for h in range(heads)], refs[2 * heads :]
     locals_, refs = refs[:heads], refs[heads:]
     norms, refs = refs[:heads], refs[heads:]
-    state_high, state_low, carried_totals, *refs = refs
+    state_high, state_low, state_rest, carried_totals, *refs = refs
     grads, scratch = refs[:heads], refs[-1]
     mine = lax.axis_index("head")
     for m, piece in enumerate(pieces):
@@ -344,12 +351,10 @@
     state = scratch[...]
     width = state.shape[0]
     totals = jnp.broadcast_to(take_totals(pieces[0], share), state.shape)
-    pair = split(state)
-    state_high[:width] = pair[0]
-    state_low[:width] = pair[1]
-    rest = split(totals)
-    state_high[width:] = rest[0]
-    state_low[width:] = rest[1]
+    parts = split3(jnp.concatenate([state, totals], axis=0))
+    for target, value in zip((state_high, state_low, state_rest), parts):
+        target[...] = value
+    pair = (parts[0][:width], parts[1][:width])
     carried = None
     for h in range(heads):
         feat = (feats[h][0][...], feats[h][1][...])
@@ -379,8 +384,8 @@
 
 
 def query_grad_body(
-    block, queries, values, key_high, key_low, feat_high, feat_low, grad_numer, grad_norm,
-    state_high, state_low, logit_ref, grad_weight, score_grad_high, score_grad_low,
+    block, queries, values, key_high, key_low, key_rest, feat_high, feat_low, grad_numer,
+    grad_norm, state_high, state_low, state_rest, logit_ref, grad_weight, score_grad_high, score_grad_low,
 ):
     rows, width = values.shape
     numer = split(grad_numer[...])
@@ -389,13 +394,13 @@
     extended = [jnp.concatenate([a, b], axis=1) for a, b in zip(numer, scaled_norm)]
     value_pair = split(values[...])
     feat = (feat_high[...], feat_low[...])
-    state = (state_high[...], state_low[...])
+    state = (state_high[...], state_low[...], state_rest[...])
     mask = causal(block)
     parts = []
     for i in range(rows // block):
         at = slice(i * block, (i + 1) * block)
         norm_part = jnp.concatenate([norm_grad[at]] * (block // width), axis=1)
-        grad_query = dot3(cut(extended, at), state, NN)
+        grad_query = dot5(cut(extended, at), state, NN)
         for j in range(i + 1):
             past = slice(j * block, (j + 1) * block)
             grad_scores = dot3(cut(numer, at), cut(value_pair, past), NT) + norm_part
@@ -404,7 +409,9 @@
             pair = split(grad_scores)
             score_grad_high[at, past] = pair[0]
             score_grad_low[at, past] = pair[1]
-            grad_query = grad_query + dot3(pair, (key_high[past], key_low[past]), NN)
+            grad_query = grad_query + dot5(
+                pair, (key_high[past], key_low[past], key_rest[past]), NN
+            )
         parts.append(logit_grad(joined(cut(feat, at)), grad_query))
     grad_logits = jnp.concatenate(parts, axis=0)
     logit_ref[...] = grad_logits
@@ -549,9 +556,9 @@
     scaled = cotangent * weight[:, None]
 
     feat_shape = out((rows, wide), BF16)
-    key_high, key_low, local = call(
+    key_high, key_low, key_rest, local = call(
         bind(key_body, share),
-        [feat_shape, feat_shape, out(message)],
+        [feat_shape] * 3 + [out(message)],
         [pltpu.with_memory_space_constraint(x, pltpu.HBM) for x in (keys, values, k_feature)],
         6 * unit,
         [hbm] * 3,
@@ -639,20 +646,21 @@
     carried_parts = [results[0]] + exchange(results[1:], peers)
     results = call(
         bind(inter_body, heads, peers, share),
-        [out((2 * width, wide), BF16)] * 2
+        [out((2 * width, wide), BF16)] * 3
         + [out((8, half))]
         + [out((rows, width))] * heads,
         (scaled, *prefix, *flat_feats, *[pair[0] for pair in inner], *norms),
         4 * heads * unit,
         scratch=[pltpu.VMEM((width, wide), F32)],
     )
-    state, carried_totals, norm_grads = results[:2], results[2], results[3:]
+    state, carried_totals, norm_grads = results[:3], results[3], results[4:]
     (carried,) = call(carried_sum_body, [out(message)], (carried_totals, *carried_parts))
 
     weight_grads, query_logits, inner_args = [], [], []
     for h in range(heads):
         args = [
-            queries, values, key_high, key_low, *feats[h], grads[h], norm_grads[h], *state,
+            queries, values, key_high, key_low, key_rest, *feats[h], grads[h], norm_grads[h],
+            *state,
         ]
         outs = [out((rows, half)), out((width, half))] + [out((rows, rows), BF16)] * 2
         logits, grad_weight, *score_grads = call(

time: 61.6 us -> 65.3 us (1.060)
  waiting for transfers between devices: 17.7 us -> 20.2 us
  Pallas kernels: 15.4 us -> 16.3 us
    ppermute x18, waiting for transfers between devices: 16.3 us -> 18.8 us  [swap(): received.append(lax.ppermute(value, ('ctx', 'head'), pairs))]
    pallas_call x23, Pallas kernels: 15.4 us -> 16.3 us  [call(): pl.pallas_call(body, out_shape=outs, scratch_shapes=scratch, cost_estimat...]
  transfers between devices with their start and end apart: 23 -> 23, of which waited for: 14 -> 13; matrix products, arithmetic and copies ran while one was open for 0% -> 0% of each run, Pallas kernels for 18% -> 18%
where the time goes in v3:
time: 65.3 us; the launch traced here: 65.1 us
  starting transfers between devices  26.6 us (41%)
  waiting for transfers between devices  20.2 us (31%)
  Pallas kernels  16.3 us (25%)
  local copies, waits for them, and re-layouts  0.93 us (1%)
  between operations  0.89 us (1%)
    ppermute x18, starting transfers between devices, swap(): received.append(lax.ppermute(value, ('ctx', 'head'), pairs))  25.3 us
    ppermute x18, waiting for transfers between devices, swap(): received.append(lax.ppermute(value, ('ctx', 'head'), pairs))  18.8 us
    pallas_call x23, Pallas kernels, call(): pl.pallas_call(body, out_shape=outs, scratch_shapes=scratch, cost_estimat...  16.3 us
    ppermute x5, waiting for transfers between devices, exchange(): lax.ppermute(value, 'head', [(i, i ^ m) for i in range(peers)])  1.36 us
  transfers between devices with their start and end apart: 23, of which 13 were waited for; matrix products, arithmetic and copies ran while one was open for 0% of the time, Pallas kernels for 18%

profile of v3, /device:TPU:0, one launch (start us, length us, event | category | flops | bytes accessed | tf_op | source)
XLA Modules:
  0.0 65.1 jit_solution(11349628130029174571)
XLA Ops:
  0.7 2.2 %shard_map.119 = (bf16[512,256]{1,0:T(8,128)(2,1)S(1)}, bf16[512,256]{1,0:T(8,128)(2,1)S(1)}, bf16[512,256]{1,0:T(8,128)(2,1)S(1)}, f32[136,128]{1,0:T(8,128)S(1)}) custom-call(f32[512,128]{1,0:T(8,128)} %keys.1, f32[512,128]{1,0:T(8,128)} %values.9, f32[128,128]{1,0:T(8,128)} %weight.5), custom_call_target="tpu_custom_call" | custom-call | flops 201326592 | bytes 2232320 | tf_op jit(solution)/shard_map/pallas_call | solution.py:154
  2.9 3.0 %collective-permute-start = (f32[136,128]{1,0:T(8,128)S(1)}, f32[136,128]{1,0:T(8,128)S(1)}, u32[]{:S(2)}, u32[]{:S(2)}) collective-permute-start(f32[136,128]{1,0:T(8,128)S(1)} %get-tuple-element.64.local), channel_id=1, source_target_pairs={{0,2},{1,9},{2,0},{3,11},{4,6},{5,13},{6,4},{7,15},{8,10},{9,1},{1... | collective-permute-start | bytes 208904 | tf_op jit(solution)/shard_map/ppermute | solution.py:130
  5.9 1.5 %collective-permute-start.1 = (f32[136,128]{1,0:T(8,128)S(1)}, f32[136,128]{1,0:T(8,128)S(1)}, u32[]{:S(2)}, u32[]{:S(2)}) collective-permute-start(f32[136,128]{1,0:T(8,128)S(1)} %get-tuple-element.64.local), channel_id=1, source_target_pairs={{0,4},{1,17},{2,6},{3,19},{4,0},{5,21},{6,2},{7,23},{8,12},{9,25},... | collective-permute-start | bytes 208904 | tf_op jit(solution)/shard_map/ppermute | solution.py:130
  8.2 2.0 %collective-permute-done.1.refs_1_ = f32[136,128]{1,0:T(8,128)S(1)} collective-permute-done((f32[136,128]{1,0:T(8,128)S(1)}, f32[136,128]{1,0:T(8,128)S(1)}, u32[]{:S(2)}, u32[]{:S(2)}) %collective-permute-start.1) | collective-permute-done | bytes 69664 | tf_op jit(solution)/shard_map/ppermute | solution.py:130
  10.2 2.4 %collective-permute-done.2.refs_2_ = f32[136,128]{1,0:T(8,128)S(1)} collective-permute-done((f32[136,128]{1,0:T(8,128)S(1)}, f32[136,128]{1,0:T(8,128)S(1)}, u32[]{:S(2)}, u32[]{:S(2)}) %collective-permute-start.2) | collective-permute-done | bytes 69664 | tf_op jit(solution)/shard_map/ppermute | solution.py:130
  12.7 1.6 %collective-permute-start.3 = (f32[136,128]{1,0:T(8,128)S(1)}, f32[136,128]{1,0:T(8,128)S(1)}, u32[]{:S(2)}, u32[]{:S(2)}) collective-permute-start(f32[136,128]{1,0:T(8,128)S(1)} %get-tuple-element.66), channel_id=1, source_target_pairs={{0,8},{1,3},{2,10},{3,1},{4,12},{5,7},{6,14},{7,5},{8,0},{9,11},{1... | collective-permute-start | bytes 208904 | tf_op jit(solution)/shard_map/ppermute | solution.py:130
  14.4 2.6 %collective-permute-start.4 = (f32[136,128]{1,0:T(8,128)S(1)}, f32[136,128]{1,0:T(8,128)S(1)}, u32[]{:S(2)}, u32[]{:S(2)}) collective-permute-start(f32[136,128]{1,0:T(8,128)S(1)} %get-tuple-element.67), channel_id=1, source_target_pairs={{0,16},{1,5},{2,18},{3,7},{4,20},{5,1},{6,22},{7,3},{8,24},{9,13},... | collective-permute-start | bytes 208904 | tf_op jit(solution)/shard_map/ppermute | solution.py:130
  18.1 1.3 %shard_map.120 = (bf16[512,256]{1,0:T(8,128)(2,1)S(1)}, bf16[512,256]{1,0:T(8,128)(2,1)S(1)}, bf16[512,512]{1,0:T(8,128)(2,1)S(1)}, bf16[512,512]{1,0:T(8,128)(2...) custom-call(f32[512,256]{1,0:T(8,128)S(1)} %copy-done, f32[2,128,128]{2,1,0:T(8,128)S(1)} %copy-done.2, ...), custom_call_target="tpu_custom_call" | custom-call | flops 301989888 | bytes 5636096 | tf_op jit(solution)/shard_map/pallas_call | solution.py:154
  19.5 1.3 %shard_map.123 = (bf16[512,256]{1,0:T(8,128)(2,1)S(1)}, bf16[512,256]{1,0:T(8,128)(2,1)S(1)}, bf16[512,512]{1,0:T(8,128)(2,1)S(1)}, bf16[512,512]{1,0:T(8,128)(2...) custom-call(f32[512,256]{1,0:T(8,128)S(1)} %copy-done, f32[2,128,128]{2,1,0:T(8,128)S(1)} %copy-done.2, ...), custom_call_target="tpu_custom_call" | custom-call | flops 301989888 | bytes 5636096 | tf_op jit(solution)/shard_map/pallas_call | solution.py:154
  20.8 2.2 %collective-permute-done.5.refs_2_ = f32[136,128]{1,0:T(8,128)S(1)} collective-permute-done((f32[136,128]{1,0:T(8,128)S(1)}, f32[136,128]{1,0:T(8,128)S(1)}, u32[]{:S(2)}, u32[]{:S(2)}) %collective-permute-start.5) | collective-permute-done | bytes 69664 | tf_op jit(solution)/shard_map/ppermute | solution.py:130
  25.9 1.4 %collective-permute-start.9 = (f32[136,128]{1,0:T(8,128)S(1)}, f32[136,128]{1,0:T(8,128)S(1)}, u32[]{:S(2)}, u32[]{:S(2)}) collective-permute-start(f32[136,128]{1,0:T(8,128)S(1)} %shard_map.129.local), channel_id=1, source_target_pairs={{0,16},{1,5},{2,18},{3,7},{4,20},{5,1},{6,22},{7,3},{8,24},{9,13},... | collective-permute-start | bytes 208904 | tf_op jit(solution)/shard_map/ppermute | solution.py:130
  27.3 3.0 %collective-permute-start.10 = (f32[136,128]{1,0:T(8,128)S(1)}, f32[136,128]{1,0:T(8,128)S(1)}, u32[]{:S(2)}, u32[]{:S(2)}) collective-permute-start(f32[136,128]{1,0:T(8,128)S(1)} %shard_map.129.local), channel_id=1, source_target_pairs={{0,24},{1,7},{2,26},{3,5},{4,28},{5,3},{6,30},{7,1},{8,16},{9,15},... | collective-permute-start | bytes 208904 | tf_op jit(solution)/shard_map/ppermute | solution.py:130
  30.2 1.9 %shard_map.126 = (f32[512,128]{1,0:T(8,128)S(1)}, f32[128,128]{1,0:T(8,128)S(1)}, bf16[512,512]{1,0:T(8,128)(2,1)S(1)}, bf16[512,512]{1,0:T(8,128)(2,1)S(1)}) custom-call(f32[512,256]{1,0:T(8,128)S(1)} %copy-done, f32[512,128]{1,0:T(8,128)S(1)} %copy-done.1, bf16[512,256]{1,0:T(8,128)(2,1)S(1)} %get-tuple-element.59.key_high, ...), custom_call_target="tpu_custom_call" | custom-call | flops 268435456 | bytes 7143424 | tf_op jit(solution)/shard_map/pallas_call | solution.py:154
  32.2 1.9 %shard_map.127 = (f32[512,128]{1,0:T(8,128)S(1)}, f32[128,128]{1,0:T(8,128)S(1)}, bf16[512,512]{1,0:T(8,128)(2,1)S(1)}, bf16[512,512]{1,0:T(8,128)(2,1)S(1)}) custom-call(f32[512,256]{1,0:T(8,128)S(1)} %copy-done, f32[512,128]{1,0:T(8,128)S(1)} %copy-done.1, bf16[512,256]{1,0:T(8,128)(2,1)S(1)} %get-tuple-element.59.key_high, ...), custom_call_target="tpu_custom_call" | custom-call | flops 268435456 | bytes 7143424 | tf_op jit(solution)/shard_map/pallas_call | solution.py:154
  35.3 2.4 %collective-permute-start.13 = (f32[200,128]{1,0:T(8,128)S(1)}, f32[200,128]{1,0:T(8,128)S(1)}, u32[]{:S(2)}, u32[]{:S(2)}) collective-permute-start(f32[200,128]{1,0:T(8,128)S(1)} %get-tuple-element.94), channel_id=1, source_target_pairs={{0,6},{1,25},{2,4},{3,27},{4,2},{5,29},{6,0},{7,31},{8,14},{9,17},... | collective-permute-start | bytes 307208 | tf_op jit(solution)/shard_map/ppermute | solution.py:130
  37.8 1.2 %shard_map.132.inner = f32[512,384]{1,0:T(8,128)S(1)} custom-call(bf16[512,256]{1,0:T(8,128)(2,1)S(1)} %get-tuple-element.62.refs_0_.refs_2_.feat_high, bf16[512,256]{1,0:T(8,128)(2,1)S(1)} %get-tuple-element.63.refs_1_.refs_3_.feat_low, bf16[512,512]{1,0:T(8,128)(2,1)S(1)} %get-tuple-element.95.refs_2_, bf16[512,512]{1,0:T(8,128)(2,1)S(1)} %get-tuple-element.96.refs_3_, ...), custom_call_target="tpu_custom_call" | custom-call | flops 402653184 | bytes 11796480 | tf_op jit(solution)/shard_map/pallas_call | solution.py:154
  39.5 1.4 %collective-permute-done.13.refs_2_ = f32[200,128]{1,0:T(8,128)S(1)} collective-permute-done((f32[200,128]{1,0:T(8,128)S(1)}, f32[200,128]{1,0:T(8,128)S(1)}, u32[]{:S(2)}, u32[]{:S(2)}) %collective-permute-start.13) | collective-permute-done | bytes 102432 | tf_op jit(solution)/shard_map/ppermute | solution.py:130
  44.0 2.7 %collective-permute-start.17 = (f32[128,128]{1,0:T(8,128)S(1)}, f32[128,128]{1,0:T(8,128)S(1)}, u32[]{:S(2)}, u32[]{:S(2)}) collective-permute-start(f32[128,128]{1,0:T(8,128)S(1)} %shard_map.137.refs_0_), channel_id=1, source_target_pairs={{0,16},{1,5},{2,18},{3,7},{4,20},{5,1},{6,22},{7,3},{8,24},{9,13},... | collective-permute-start | bytes 196616 | tf_op jit(solution)/shard_map/ppermute | solution.py:130
  46.7 1.6 %collective-permute-start.18 = (f32[128,128]{1,0:T(8,128)S(1)}, f32[128,128]{1,0:T(8,128)S(1)}, u32[]{:S(2)}, u32[]{:S(2)}) collective-permute-start(f32[128,128]{1,0:T(8,128)S(1)} %shard_map.137.refs_0_), channel_id=1, source_target_pairs={{0,24},{1,7},{2,26},{3,5},{4,28},{5,3},{6,30},{7,1},{8,16},{9,15},... | collective-permute-start | bytes 196616 | tf_op jit(solution)/shard_map/ppermute | solution.py:130
  49.2 3.6 %collective-permute-done.18.refs_3_ = f32[128,128]{1,0:T(8,128)S(1)} collective-permute-done((f32[128,128]{1,0:T(8,128)S(1)}, f32[128,128]{1,0:T(8,128)S(1)}, u32[]{:S(2)}, u32[]{:S(2)}) %collective-permute-start.18) | collective-permute-done | bytes 65568 | tf_op jit(solution)/shard_map/ppermute | solution.py:130
  52.8 1.6 %collective-permute-start.19 = (f32[128,128]{1,0:T(8,128)S(1)}, f32[128,128]{1,0:T(8,128)S(1)}, u32[]{:S(2)}, u32[]{:S(2)}) collective-permute-start(f32[128,128]{1,0:T(8,128)S(1)} %shard_map.138.refs_0_), channel_id=1, source_target_pairs={{0,2},{1,9},{2,0},{3,11},{4,6},{5,13},{6,4},{7,15},{8,10},{9,1},{1... | collective-permute-start | bytes 196616 | tf_op jit(solution)/shard_map/ppermute | solution.py:130
  54.4 2.2 %collective-permute-start.20 = (f32[128,128]{1,0:T(8,128)S(1)}, f32[128,128]{1,0:T(8,128)S(1)}, u32[]{:S(2)}, u32[]{:S(2)}) collective-permute-start(f32[128,128]{1,0:T(8,128)S(1)} %shard_map.138.refs_0_), channel_id=1, source_target_pairs={{0,4},{1,17},{2,6},{3,19},{4,0},{5,21},{6,2},{7,23},{8,12},{9,25},... | collective-permute-start | bytes 196616 | tf_op jit(solution)/shard_map/ppermute | solution.py:130
  57.1 1.7 %collective-permute-done.20.refs_2_ = f32[128,128]{1,0:T(8,128)S(1)} collective-permute-done((f32[128,128]{1,0:T(8,128)S(1)}, f32[128,128]{1,0:T(8,128)S(1)}, u32[]{:S(2)}, u32[]{:S(2)}) %collective-permute-start.20) | collective-permute-done | bytes 65568 | tf_op jit(solution)/shard_map/ppermute | solution.py:130
  58.9 2.9 %collective-permute-done.21.refs_3_ = f32[128,128]{1,0:T(8,128)S(1)} collective-permute-done((f32[128,128]{1,0:T(8,128)S(1)}, f32[128,128]{1,0:T(8,128)S(1)}, u32[]{:S(2)}, u32[]{:S(2)}) %collective-permute-start.21) | collective-permute-done | bytes 65568 | tf_op jit(solution)/shard_map/ppermute | solution.py:130
  (63 shorter events, 14.1 us)
Async XLA Ops:
  0.6 16.6 %copy-start.5 = (f32[512,256]{1,0:T(8,128)S(1)}, f32[512,256]{1,0:T(8,128)}, u32[]{:S(2)}) copy-start(f32[512,256]{1,0:T(8,128)} %param.11) | copy-start | bytes 1572868
  2.9 5.3 %collective-permute-start = (f32[136,128]{1,0:T(8,128)S(1)}, f32[136,128]{1,0:T(8,128)S(1)}, u32[]{:S(2)}, u32[]{:S(2)}) collective-permute-start(f32[136,128]{1,0:T(8,128)S(1)} %get-tuple-element.64.local), channel_id=1, source_target_pairs={{0,2},{1,9},{2,0},{3,11},{4,6},{5,13},{6,4},{7,15},{8,10},{9,1},{1... | collective-permute-start | bytes 208904 | tf_op jit(solution)/shard_map/ppermute | solution.py:130
  5.9 4.3 %collective-permute-start.1 = (f32[136,128]{1,0:T(8,128)S(1)}, f32[136,128]{1,0:T(8,128)S(1)}, u32[]{:S(2)}, u32[]{:S(2)}) collective-permute-start(f32[136,128]{1,0:T(8,128)S(1)} %get-tuple-element.64.local), channel_id=1, source_target_pairs={{0,4},{1,17},{2,6},{3,19},{4,0},{5,21},{6,2},{7,23},{8,12},{9,25},... | collective-permute-start | bytes 208904 | tf_op jit(solution)/shard_map/ppermute | solution.py:130
  7.5 5.2 %collective-permute-start.2 = (f32[136,128]{1,0:T(8,128)S(1)}, f32[136,128]{1,0:T(8,128)S(1)}, u32[]{:S(2)}, u32[]{:S(2)}) collective-permute-start(f32[136,128]{1,0:T(8,128)S(1)} %get-tuple-element.64.local), channel_id=1, source_target_pairs={{0,6},{1,25},{2,4},{3,27},{4,2},{5,29},{6,0},{7,31},{8,14},{9,17},... | collective-permute-start | bytes 208904 | tf_op jit(solution)/shard_map/ppermute | solution.py:130
  12.7 8.1 %collective-permute-start.3 = (f32[136,128]{1,0:T(8,128)S(1)}, f32[136,128]{1,0:T(8,128)S(1)}, u32[]{:S(2)}, u32[]{:S(2)}) collective-permute-start(f32[136,128]{1,0:T(8,128)S(1)} %get-tuple-element.66), channel_id=1, source_target_pairs={{0,8},{1,3},{2,10},{3,1},{4,12},{5,7},{6,14},{7,5},{8,0},{9,11},{1... | collective-permute-start | bytes 208904 | tf_op jit(solution)/shard_map/ppermute | solution.py:130
  14.4 6.4 %collective-permute-start.4 = (f32[136,128]{1,0:T(8,128)S(1)}, f32[136,128]{1,0:T(8,128)S(1)}, u32[]{:S(2)}, u32[]{:S(2)}) collective-permute-start(f32[136,128]{1,0:T(8,128)S(1)} %get-tuple-element.67), channel_id=1, source_target_pairs={{0,16},{1,5},{2,18},{3,7},{4,20},{5,1},{6,22},{7,3},{8,24},{9,13},... | collective-permute-start | bytes 208904 | tf_op jit(solution)/shard_map/ppermute | solution.py:130
  17.0 6.1 %collective-permute-start.5 = (f32[136,128]{1,0:T(8,128)S(1)}, f32[136,128]{1,0:T(8,128)S(1)}, u32[]{:S(2)}, u32[]{:S(2)}) collective-permute-start(f32[136,128]{1,0:T(8,128)S(1)} %get-tuple-element.68), channel_id=1, source_target_pairs={{0,24},{1,7},{2,26},{3,5},{4,28},{5,3},{6,30},{7,1},{8,16},{9,15},... | collective-permute-start | bytes 208904 | tf_op jit(solution)/shard_map/ppermute | solution.py:130
  23.1 1.8 %collective-permute-start.6 = (f32[136,128]{1,0:T(8,128)S(1)}, f32[136,128]{1,0:T(8,128)S(1)}, u32[]{:S(2)}, u32[]{:S(2)}) collective-permute-start(f32[136,128]{1,0:T(8,128)S(1)} %shard_map.122.before.refs_0_), channel_id=1, source_target_pairs={{0,1},{1,0},{2,3},{3,2},{4,5},{5,4},{6,7},{7,6},{8,9},{9,8},{10,11... | collective-permute-start | bytes 208904 | tf_op jit(solution)/shard_map/ppermute | solution.py:138
  24.3 1.5 %collective-permute-start.7 = (f32[128,128]{1,0:T(8,128)S(1)}, f32[128,128]{1,0:T(8,128)S(1)}, u32[]{:S(2)}, u32[]{:S(2)}) collective-permute-start(f32[128,128]{1,0:T(8,128)S(1)} %get-tuple-element.88), channel_id=1, source_target_pairs={{0,1},{1,0},{2,3},{3,2},{4,5},{5,4},{6,7},{7,6},{8,9},{9,8},{10,11... | collective-permute-start | bytes 196616 | tf_op jit(solution)/shard_map/ppermute | solution.py:138
  25.8 8.3 %collective-permute-start.8 = (f32[136,128]{1,0:T(8,128)S(1)}, f32[136,128]{1,0:T(8,128)S(1)}, u32[]{:S(2)}, u32[]{:S(2)}) collective-permute-start(f32[136,128]{1,0:T(8,128)S(1)} %shard_map.129.local), channel_id=1, source_target_pairs={{0,8},{1,3},{2,10},{3,1},{4,12},{5,7},{6,14},{7,5},{8,0},{9,11},{1... | collective-permute-start | bytes 208904 | tf_op jit(solution)/shard_map/ppermute | solution.py:130
  25.9 8.3 %collective-permute-start.9 = (f32[136,128]{1,0:T(8,128)S(1)}, f32[136,128]{1,0:T(8,128)S(1)}, u32[]{:S(2)}, u32[]{:S(2)}) collective-permute-start(f32[136,128]{1,0:T(8,128)S(1)} %shard_map.129.local), channel_id=1, source_target_pairs={{0,16},{1,5},{2,18},{3,7},{4,20},{5,1},{6,22},{7,3},{8,24},{9,13},... | collective-permute-start | bytes 208904 | tf_op jit(solution)/shard_map/ppermute | solution.py:130
  27.3 6.9 %collective-permute-start.10 = (f32[136,128]{1,0:T(8,128)S(1)}, f32[136,128]{1,0:T(8,128)S(1)}, u32[]{:S(2)}, u32[]{:S(2)}) collective-permute-start(f32[136,128]{1,0:T(8,128)S(1)} %shard_map.129.local), channel_id=1, source_target_pairs={{0,24},{1,7},{2,26},{3,5},{4,28},{5,3},{6,30},{7,1},{8,16},{9,15},... | collective-permute-start | bytes 208904 | tf_op jit(solution)/shard_map/ppermute | solution.py:130
  34.2 4.8 %collective-permute-start.11 = (f32[200,128]{1,0:T(8,128)S(1)}, f32[200,128]{1,0:T(8,128)S(1)}, u32[]{:S(2)}, u32[]{:S(2)}) collective-permute-start(f32[200,128]{1,0:T(8,128)S(1)} %get-tuple-element.92), channel_id=1, source_target_pairs={{0,2},{1,9},{2,0},{3,11},{4,6},{5,13},{6,4},{7,15},{8,10},{9,1},{1... | collective-permute-start | bytes 307208 | tf_op jit(solution)/shard_map/ppermute | solution.py:130
  34.8 4.7 %collective-permute-start.12 = (f32[200,128]{1,0:T(8,128)S(1)}, f32[200,128]{1,0:T(8,128)S(1)}, u32[]{:S(2)}, u32[]{:S(2)}) collective-permute-start(f32[200,128]{1,0:T(8,128)S(1)} %get-tuple-element.93), channel_id=1, source_target_pairs={{0,4},{1,17},{2,6},{3,19},{4,0},{5,21},{6,2},{7,23},{8,12},{9,25},... | collective-permute-start | bytes 307208 | tf_op jit(solution)/shard_map/ppermute | solution.py:130
  35.3 5.6 %collective-permute-start.13 = (f32[200,128]{1,0:T(8,128)S(1)}, f32[200,128]{1,0:T(8,128)S(1)}, u32[]{:S(2)}, u32[]{:S(2)}) collective-permute-start(f32[200,128]{1,0:T(8,128)S(1)} %get-tuple-element.94), channel_id=1, source_target_pairs={{0,6},{1,25},{2,4},{3,27},{4,2},{5,29},{6,0},{7,31},{8,14},{9,17},... | collective-permute-start | bytes 307208 | tf_op jit(solution)/shard_map/ppermute | solution.py:130
  42.2 22.1 %collective-permute-start.14 = (f32[256,256]{1,0:T(8,128)S(1)}, f32[256,256]{1,0:T(8,128)S(1)}, u32[]{:S(2)}, u32[]{:S(2)}) collective-permute-start(f32[256,256]{1,0:T(8,128)S(1)} %get-tuple-element.107), channel_id=1, source_target_pairs={{0,1},{1,0},{2,3},{3,2},{4,5},{5,4},{6,7},{7,6},{8,9},{9,8},{10,11... | collective-permute-start | bytes 786440 | tf_op jit(solution)/shard_map/ppermute | solution.py:138
  42.3 1.6 %collective-permute-start.15 = (f32[64,128]{1,0:T(8,128)S(1)}, f32[64,128]{1,0:T(8,128)S(1)}, u32[]{:S(2)}, u32[]{:S(2)}) collective-permute-start(f32[64,128]{1,0:T(8,128)S(1)} %get-tuple-element.111), channel_id=1, source_target_pairs={{0,1},{1,0},{2,3},{3,2},{4,5},{5,4},{6,7},{7,6},{8,9},{9,8},{10,11... | collective-permute-start | bytes 98312 | tf_op jit(solution)/shard_map/ppermute | solution.py:138
  43.9 4.5 %collective-permute-start.16 = (f32[128,128]{1,0:T(8,128)S(1)}, f32[128,128]{1,0:T(8,128)S(1)}, u32[]{:S(2)}, u32[]{:S(2)}) collective-permute-start(f32[128,128]{1,0:T(8,128)S(1)} %shard_map.137.refs_0_), channel_id=1, source_target_pairs={{0,8},{1,3},{2,10},{3,1},{4,12},{5,7},{6,14},{7,5},{8,0},{9,11},{1... | collective-permute-start | bytes 196616 | tf_op jit(solution)/shard_map/ppermute | solution.py:130
  44.0 5.2 %collective-permute-start.17 = (f32[128,128]{1,0:T(8,128)S(1)}, f32[128,128]{1,0:T(8,128)S(1)}, u32[]{:S(2)}, u32[]{:S(2)}) collective-permute-start(f32[128,128]{1,0:T(8,128)S(1)} %shard_map.137.refs_0_), channel_id=1, source_target_pairs={{0,16},{1,5},{2,18},{3,7},{4,20},{5,1},{6,22},{7,3},{8,24},{9,13},... | collective-permute-start | bytes 196616 | tf_op jit(solution)/shard_map/ppermute | solution.py:130
  46.7 6.1 %collective-permute-start.18 = (f32[128,128]{1,0:T(8,128)S(1)}, f32[128,128]{1,0:T(8,128)S(1)}, u32[]{:S(2)}, u32[]{:S(2)}) collective-permute-start(f32[128,128]{1,0:T(8,128)S(1)} %shard_map.137.refs_0_), channel_id=1, source_target_pairs={{0,24},{1,7},{2,26},{3,5},{4,28},{5,3},{6,30},{7,1},{8,16},{9,15},... | collective-permute-start | bytes 196616 | tf_op jit(solution)/shard_map/ppermute | solution.py:130
  52.8 4.3 %collective-permute-start.19 = (f32[128,128]{1,0:T(8,128)S(1)}, f32[128,128]{1,0:T(8,128)S(1)}, u32[]{:S(2)}, u32[]{:S(2)}) collective-permute-start(f32[128,128]{1,0:T(8,128)S(1)} %shard_map.138.refs_0_), channel_id=1, source_target_pairs={{0,2},{1,9},{2,0},{3,11},{4,6},{5,13},{6,4},{7,15},{8,10},{9,1},{1... | collective-permute-start | bytes 196616 | tf_op jit(solution)/shard_map/ppermute | solution.py:130
  54.4 4.5 %collective-permute-start.20 = (f32[128,128]{1,0:T(8,128)S(1)}, f32[128,128]{1,0:T(8,128)S(1)}, u32[]{:S(2)}, u32[]{:S(2)}) collective-permute-start(f32[128,128]{1,0:T(8,128)S(1)} %shard_map.138.refs_0_), channel_id=1, source_target_pairs={{0,4},{1,17},{2,6},{3,19},{4,0},{5,21},{6,2},{7,23},{8,12},{9,25},... | collective-permute-start | bytes 196616 | tf_op jit(solution)/shard_map/ppermute | solution.py:130
  56.6 5.2 %collective-permute-start.21 = (f32[128,128]{1,0:T(8,128)S(1)}, f32[128,128]{1,0:T(8,128)S(1)}, u32[]{:S(2)}, u32[]{:S(2)}) collective-permute-start(f32[128,128]{1,0:T(8,128)S(1)} %shard_map.138.refs_0_), channel_id=1, source_target_pairs={{0,6},{1,25},{2,4},{3,27},{4,2},{5,29},{6,0},{7,31},{8,14},{9,17},... | collective-permute-start | bytes 196616 | tf_op jit(solution)/shard_map/ppermute | solution.py:130
  61.8 1.9 %collective-permute-start.22 = (f32[64,128]{1,0:T(8,128)S(1)}, f32[64,128]{1,0:T(8,128)S(1)}, u32[]{:S(2)}, u32[]{:S(2)}) collective-permute-start(f32[64,128]{1,0:T(8,128)S(1)} %shard_map.140.refs_0_), channel_id=1, source_target_pairs={{0,1},{1,0},{2,3},{3,2},{4,5},{5,4},{6,7},{7,6},{8,9},{9,8},{10,11... | collective-permute-start | bytes 98312 | tf_op jit(solution)/shard_map/ppermute | solution.py:138
  (7 other events, 17.5 us)
